TPU v7x, 512 devices: a whole 4x4x16 slice. The times are simulated.
512 devices in a mesh: pipe: 8 (over x, y_hi), dp: 64 (over z, y_lo, core).
Axes of the slice: x: 4, y: 4 (y_hi: 2, y_lo: 2; y = y_hi * 2 + y_lo), z: 16, core: 2. Of those that a mesh axis runs over, the one named last changes fastest.
Arguments:
- saved: bfloat16 [8, 2, 64, 128, 1536], P('pipe', None, 'dp'), may hold values from -6 to 6
- out_grad: bfloat16 [2, 64, 128, 1536], P(None, 'dp'), may hold values from -16 to 16
- lengths: int32 [2, 64], P(None, 'dp'), may hold values from 1 to 128, 5120 in all within a row
- kernel: bfloat16 [8, 31, 1536], P('pipe'), may hold values from -1 to 1
- gain: float32 [8, 1536], P('pipe'), may hold values from 0.5 to 1.5
- bias: float32 [8, 1536], P('pipe'), may hold values from -3 to 3
Outputs:
- in_grads: bfloat16 [8, 2, 64, 128, 1536], P('pipe', None, 'dp')
- kernel_grad: float32 [8, 31, 1536], P('pipe', None, 'dp')
- gain_grad: float32 [8, 1536], P('pipe', 'dp')
- bias_grad: float32 [8, 1536], P('pipe', 'dp')
Inputs may be any that keep to these rules, and one draw needn't show every extreme that they name: In every micro-batch the lengths sum to 64 * 128 * 5 // 8 and one reaches 128.
All inputs are finite; a program needn't handle non-finite values. No bound on the sum of `lengths` on one device may be relied on, other than what follows from the above.
Results may differ from a plain program's by a relative error of at most 0.0079.
Values may be sent and summed in bfloat16 or wider, within the bound.
No kernel may reach another device: no remote copies, remote signals or barrier semaphores. Data moves between devices by JAX's collectives and lax.ppermute only.
A program may use at most 64 MiB of HBM per device.

v0:
```python
import jax
import jax.numpy as jnp
from jax import lax
from jax.sharding import PartitionSpec as P

KW = 31
MB = 2


def passed_along(value, axis, steps):
    count = lax.axis_size(axis)
    leading, last = (max(0, -steps), min(count, count - steps))
    return lax.ppermute(value, axis, [(source, source + steps) for source in range(leading, last)])


def backward_frames(x, dy, length, weights, gain, bias):
    frames = x.shape[0]
    half = (KW - 1) // 2
    mask = (jnp.arange(frames, dtype=jnp.int32) < length)[:, None]
    xm = jnp.where(mask, x.astype(jnp.float32), jnp.zeros((), jnp.float32))
    padded = jnp.pad(xm, ((half, half), (0, 0)))
    h = jnp.zeros_like(xm)
    for j in range(KW):
        h = h + weights[j] * padded[j : j + frames]
    mu = jnp.mean(h, -1, keepdims=True)
    centred = h - mu
    recip = lax.rsqrt(jnp.mean(centred * centred, -1, keepdims=True) + 1e-05)
    normed = centred * recip
    u = normed * gain + bias
    incoming = dy.astype(jnp.float32)
    dv = jnp.where(mask, incoming, jnp.zeros((), jnp.float32))
    sig = jax.nn.sigmoid(u)
    du = dv * sig * (1.0 + u * (1.0 - sig))
    dnorm = du * gain
    dh = recip * (
        dnorm
        - jnp.mean(dnorm, -1, keepdims=True)
        - normed * jnp.mean(dnorm * normed, -1, keepdims=True)
    )
    kgrad = jnp.stack([jnp.sum(dh * padded[j : j + frames], 0) for j in range(KW)], 0)
    dpad = jnp.pad(dh, ((half, half), (0, 0)))
    back = jnp.zeros_like(xm)
    for j in range(KW):
        back = back + weights[j] * dpad[KW - 1 - j : KW - 1 - j + frames]
    dx = jnp.where(mask, incoming + back, jnp.zeros((), jnp.float32)).astype(jnp.bfloat16)
    return (dx, kgrad, jnp.sum(du * normed, 0), jnp.sum(du, 0))


def local(saved, out_grad, lengths, kernel, gain, bias):
    sections = lax.axis_size("pipe")
    section = lax.axis_index("pipe")
    weights = kernel[0].astype(jnp.float32)
    gain_row = gain[0]
    bias_row = bias[0]
    x_all = saved[0, :, 0]
    dy_all = out_grad[:, 0]
    lens = lengths[:, 0]
    frames = x_all.shape[1]
    width = x_all.shape[2]
    zero_k = jnp.zeros((KW, width), jnp.float32)
    zero_c = jnp.zeros((width,), jnp.float32)

    def single(x, dy, length):
        return backward_frames(x, dy, length, weights, gain_row, bias_row)

    def advance(step, carry):
        received, outbuf, kacc, gacc, bacc = carry
        item = step - (sections - 1 - section)
        valid = jnp.logical_and(item >= 0, item < MB)
        slot = jnp.clip(item, 0, MB - 1)
        x_here = lax.dynamic_index_in_dim(x_all, slot, 0, keepdims=False)
        dy_here = lax.dynamic_index_in_dim(dy_all, slot, 0, keepdims=False)
        length = lax.dynamic_index_in_dim(lens, slot, 0, keepdims=False)
        incoming = jnp.where(section == sections - 1, dy_here, received)

        def active(operands):
            return single(operands[0], operands[1], operands[2])

        def resting(operands):
            return (jnp.zeros((frames, width), jnp.bfloat16), zero_k, zero_c, zero_c)

        dx, kg, gs, bs = lax.cond(valid, active, resting, (x_here, incoming, length))
        current = lax.dynamic_index_in_dim(outbuf, slot, 0, keepdims=False)
        outbuf = lax.dynamic_update_index_in_dim(outbuf, jnp.where(valid, dx, current), slot, 0)
        received = passed_along(dx, "pipe", -1)
        return (received, outbuf, kacc + kg, gacc + gs, bacc + bs)

    start = (
        jnp.zeros((frames, width), jnp.bfloat16),
        jnp.zeros((MB, frames, width), jnp.bfloat16),
        zero_k,
        zero_c,
        zero_c,
    )
    received, outbuf, kacc, gacc, bacc = lax.fori_loop(0, sections + MB - 1, advance, start)
    kernel_part, gain_part, bias_part = (
        lax.psum_scatter(kacc, "dp", scatter_dimension=1, tiled=True),
        lax.psum_scatter(gacc[None], "dp", scatter_dimension=1, tiled=True),
        lax.psum_scatter(bacc[None], "dp", scatter_dimension=1, tiled=True),
    )
    return (outbuf[None, :, None], kernel_part[None], gain_part, bias_part)


def solution(mesh):
    return jax.shard_map(
        local,
        mesh=mesh,
        in_specs=(
            P("pipe", None, "dp", None, None),
            P(None, "dp", None, None),
            P(None, "dp"),
            P("pipe", None, None),
            P("pipe", None),
            P("pipe", None),
        ),
        out_specs=(
            P("pipe", None, "dp", None, None),
            P("pipe", None, "dp"),
            P("pipe", "dp"),
            P("pipe", "dp"),
        ),
        check_vma=False,
    )
```

profile of v0, /device:TPU:1, one launch (start us, length us, event | category | flops | bytes accessed | tf_op | source)
XLA Modules:
  0.0 559.5 jit_solution(3583514990574385766)
XLA Ops:
  7.2 1.6 bitcast_convert_fusion
  8.8 0.9 broadcast_in_dim.67
  9.8 308.5 %while.24 = (s32[]{:T(128)}, bf16[128,1536]{1,0:T(8,128)(2,1)S(1)}, bf16[2,128,1536]{2,1,0:T(8,128)(2,1)}, f32[31,1536]{1,0:T(8,128)S(1)}, f32[1536]{0:T(1024)},...) while((s32[]{:T(128)}, bf16[128,1536]{1,0:T(8,128)(2,1)S(1)}, ...), condition=%wide.region_40.41_spmd.clone, body=%wide.region_0.40_spmd.clone.sunk | while | flops 44680968 | bytes 33013140 | solution.py:95
  9.8 1.3 conditional.3
  11.1 1.4 collective-permute-start
  12.5 1.0 constant_dynamic-slice_fusion.4
  14.3 0.7 select_add_fusion.6
  15.6 6.4 %collective-permute-done = bf16[128,1536]{1,0:T(8,128)(2,1)S(1)} collective-permute-done((bf16[128,1536]{1,0:T(8,128)(2,1)S(1)}, bf16[128,1536]{1,0:T(8,128)(2,1)S(1)}, u32[]{:S(2)}, u32[]{:S(2)}) %collective-permute-start) | collective-permute-done | bytes 393248 | tf_op jit(solution)/shard_map/while/body/eval_jaxpr/ppermute | solution.py:13
  22.0 1.3 conditional.3
  23.3 1.4 collective-permute-start
  24.7 1.0 constant_dynamic-slice_fusion.4
  27.8 11.0 %collective-permute-done = bf16[128,1536]{1,0:T(8,128)(2,1)S(1)} collective-permute-done((bf16[128,1536]{1,0:T(8,128)(2,1)S(1)}, bf16[128,1536]{1,0:T(8,128)(2,1)S(1)}, u32[]{:S(2)}, u32[]{:S(2)}) %collective-permute-start) | collective-permute-done | bytes 393248 | tf_op jit(solution)/shard_map/while/body/eval_jaxpr/ppermute | solution.py:13
  38.8 1.3 conditional.3
  40.0 1.4 collective-permute-start
  41.5 1.0 constant_dynamic-slice_fusion.4
  44.5 9.9 %collective-permute-done = bf16[128,1536]{1,0:T(8,128)(2,1)S(1)} collective-permute-done((bf16[128,1536]{1,0:T(8,128)(2,1)S(1)}, bf16[128,1536]{1,0:T(8,128)(2,1)S(1)}, u32[]{:S(2)}, u32[]{:S(2)}) %collective-permute-start) | collective-permute-done | bytes 393248 | tf_op jit(solution)/shard_map/while/body/eval_jaxpr/ppermute | solution.py:13
  54.4 1.3 conditional.3
  55.7 1.4 collective-permute-start
  57.1 1.0 constant_dynamic-slice_fusion.4
  60.2 7.3 %collective-permute-done = bf16[128,1536]{1,0:T(8,128)(2,1)S(1)} collective-permute-done((bf16[128,1536]{1,0:T(8,128)(2,1)S(1)}, bf16[128,1536]{1,0:T(8,128)(2,1)S(1)}, u32[]{:S(2)}, u32[]{:S(2)}) %collective-permute-start) | collective-permute-done | bytes 393248 | tf_op jit(solution)/shard_map/while/body/eval_jaxpr/ppermute | solution.py:13
  67.5 1.3 conditional.3
  68.8 1.4 collective-permute-start
  70.2 1.0 constant_dynamic-slice_fusion.4
  73.3 6.3 %collective-permute-done = bf16[128,1536]{1,0:T(8,128)(2,1)S(1)} collective-permute-done((bf16[128,1536]{1,0:T(8,128)(2,1)S(1)}, bf16[128,1536]{1,0:T(8,128)(2,1)S(1)}, u32[]{:S(2)}, u32[]{:S(2)}) %collective-permute-start) | collective-permute-done | bytes 393248 | tf_op jit(solution)/shard_map/while/body/eval_jaxpr/ppermute | solution.py:13
  79.6 1.3 conditional.3
  80.8 1.4 collective-permute-start
  82.2 1.0 constant_dynamic-slice_fusion.4
  85.3 6.5 %collective-permute-done = bf16[128,1536]{1,0:T(8,128)(2,1)S(1)} collective-permute-done((bf16[128,1536]{1,0:T(8,128)(2,1)S(1)}, bf16[128,1536]{1,0:T(8,128)(2,1)S(1)}, u32[]{:S(2)}, u32[]{:S(2)}) %collective-permute-start) | collective-permute-done | bytes 393248 | tf_op jit(solution)/shard_map/while/body/eval_jaxpr/ppermute | solution.py:13
  91.9 1.3 conditional.3
  93.1 1.4 collective-permute-start
  94.5 1.0 constant_dynamic-slice_fusion.4
  97.6 153.0 %collective-permute-done = bf16[128,1536]{1,0:T(8,128)(2,1)S(1)} collective-permute-done((bf16[128,1536]{1,0:T(8,128)(2,1)S(1)}, bf16[128,1536]{1,0:T(8,128)(2,1)S(1)}, u32[]{:S(2)}, u32[]{:S(2)}) %collective-permute-start) | collective-permute-done | bytes 393248 | tf_op jit(solution)/shard_map/while/body/eval_jaxpr/ppermute | solution.py:13
  250.6 23.2 %conditional.3 = (bf16[128,1536]{1,0:T(8,128)(2,1)S(1)}, f32[31,1536]{1,0:T(8,128)S(1)}, f32[1536]{0:T(1024)}, f32[1536]{0:T(1024)}) conditional(s32[]{:T(128)} %convert_element_type.54, () %tuple.129, (s32[2]{0:T(128)}, s32[]{:T(128)}, pred[]{:T(512)}, bf16[2,128,1536]{2,1,0:T(8,128)(2,1)}, bf16[128,1536]{1,0:T(8,128)(2,1)S(1)}, ...), branch_computations={%region_1.1_spmd, %region_2.39_spmd} | conditional | flops 44382976 | bytes 22475666 | solution.py:82
  250.6 1.8 slice_reduce_fusion.30
  252.6 1.2 dynamic_slice.44
  254.5 1.1 convert_select_fusion.1
  255.7 1.4 slice_reduce_fusion.29
  257.6 3.2 fusion.65
  261.2 0.7 reduce.31
  262.6 2.4 multiply_reduce_fusion
  265.0 2.5 multiply_reduce_fusion.1
  267.7 1.5 multiply_reduce_fusion.20
  270.6 3.2 fusion.3
  273.8 1.4 collective-permute-start
  275.3 1.0 constant_dynamic-slice_fusion.4
  278.3 6.5 %collective-permute-done = bf16[128,1536]{1,0:T(8,128)(2,1)S(1)} collective-permute-done((bf16[128,1536]{1,0:T(8,128)(2,1)S(1)}, bf16[128,1536]{1,0:T(8,128)(2,1)S(1)}, u32[]{:S(2)}, u32[]{:S(2)}) %collective-permute-start) | collective-permute-done | bytes 393248 | tf_op jit(solution)/shard_map/while/body/eval_jaxpr/ppermute | solution.py:13
  284.9 23.2 %conditional.3 = (bf16[128,1536]{1,0:T(8,128)(2,1)S(1)}, f32[31,1536]{1,0:T(8,128)S(1)}, f32[1536]{0:T(1024)}, f32[1536]{0:T(1024)}) conditional(s32[]{:T(128)} %convert_element_type.54, () %tuple.129, (s32[2]{0:T(128)}, s32[]{:T(128)}, pred[]{:T(512)}, bf16[2,128,1536]{2,1,0:T(8,128)(2,1)}, bf16[128,1536]{1,0:T(8,128)(2,1)S(1)}, ...), branch_computations={%region_1.1_spmd, %region_2.39_spmd} | conditional | flops 44382976 | bytes 22475666 | solution.py:82
  284.9 1.8 slice_reduce_fusion.30
  286.9 1.2 dynamic_slice.44
  288.8 1.1 convert_select_fusion.1
  289.9 1.4 slice_reduce_fusion.29
  291.9 3.2 fusion.65
  295.4 0.7 reduce.31
  296.9 2.4 multiply_reduce_fusion
  299.3 2.5 multiply_reduce_fusion.1
  302.0 1.5 multiply_reduce_fusion.20
  304.9 3.2 fusion.3
  308.1 1.4 collective-permute-start
  309.5 1.0 constant_dynamic-slice_fusion.4
  312.6 5.6 %collective-permute-done = bf16[128,1536]{1,0:T(8,128)(2,1)S(1)} collective-permute-done((bf16[128,1536]{1,0:T(8,128)(2,1)S(1)}, bf16[128,1536]{1,0:T(8,128)(2,1)S(1)}, u32[]{:S(2)}, u32[]{:S(2)}) %collective-permute-start) | collective-permute-done | bytes 393248 | tf_op jit(solution)/shard_map/while/body/eval_jaxpr/ppermute | solution.py:13
  318.3 1.2 copy.11
  320.9 1.3 dynamic-slice
  322.8 216.3 %all-reduce.5 = (f32[1,1536]{1,0:T(1,128)S(1)}, f32[1,1536]{1,0:T(1,128)S(1)}) all-reduce(f32[1,1536]{1,0:T(1,128)S(1)} %broadcast_in_dim.72, f32[1,1536]{1,0:T(1,128)S(1)} %broadcast_in_dim.73), channel_id=3, replica_groups=mesh['pipe'=8,'dp'=64] {'dp'}, use_global_device_ids=true, to_apply=%region_42.43.clone | all-reduce | flops 3072 | bytes 24576
  539.6 13.0 %reduce-scatter.7.cloned.1.call-done = f32[31,24]{0,1:T(8,128)} async-done(((f32[31,1536]{0,1:T(8,128)}), f32[31,24]{0,1:T(8,128)}) %reduce-scatter.7.cloned.1.call-update) | async-done | bytes 2992
  (499 shorter events, 33.9 us)
Async XLA Ops:
  7.2 545.5 %reduce-scatter.7.cloned.1.call-start = ((), (), s32[]{:S(2)}) async-start(), calls=%async_computation.1 | async-start | bytes 798720
  11.1 10.9 %collective-permute-start = (bf16[128,1536]{1,0:T(8,128)(2,1)S(1)}, bf16[128,1536]{1,0:T(8,128)(2,1)S(1)}, u32[]{:S(2)}, u32[]{:S(2)}) collective-permute-start(bf16[128,1536]{1,0:T(8,128)(2,1)S(1)} %get-tuple-element.642), channel_id=1, source_target_pairs={{64,0},{128,64},{192,128},{256,192},{320,256},{384,320},{448,384},... | collective-permute-start | bytes 1179656 | tf_op jit(solution)/shard_map/while/body/eval_jaxpr/ppermute | solution.py:13
  13.7 8.3 %copy-start.3 = (bf16[2,128,1536]{2,1,0:T(8,128)(2,1)}, bf16[2,128,1536]{2,1,0:T(8,128)(2,1)S(1)}, u32[]{:S(2)}) copy-start(bf16[2,128,1536]{2,1,0:T(8,128)(2,1)S(1)} %bitcast_dynamic-update-slice_fusion.2) | copy-start | bytes 2359300 | tf_op jit(solution)/shard_map/while
  23.3 15.5 %collective-permute-start = (bf16[128,1536]{1,0:T(8,128)(2,1)S(1)}, bf16[128,1536]{1,0:T(8,128)(2,1)S(1)}, u32[]{:S(2)}, u32[]{:S(2)}) collective-permute-start(bf16[128,1536]{1,0:T(8,128)(2,1)S(1)} %get-tuple-element.642), channel_id=1, source_target_pairs={{64,0},{128,64},{192,128},{256,192},{320,256},{384,320},{448,384},... | collective-permute-start | bytes 1179656 | tf_op jit(solution)/shard_map/while/body/eval_jaxpr/ppermute | solution.py:13
  25.9 12.9 %copy-start.3 = (bf16[2,128,1536]{2,1,0:T(8,128)(2,1)}, bf16[2,128,1536]{2,1,0:T(8,128)(2,1)S(1)}, u32[]{:S(2)}) copy-start(bf16[2,128,1536]{2,1,0:T(8,128)(2,1)S(1)} %bitcast_dynamic-update-slice_fusion.2) | copy-start | bytes 2359300 | tf_op jit(solution)/shard_map/while
  40.0 14.4 %collective-permute-start = (bf16[128,1536]{1,0:T(8,128)(2,1)S(1)}, bf16[128,1536]{1,0:T(8,128)(2,1)S(1)}, u32[]{:S(2)}, u32[]{:S(2)}) collective-permute-start(bf16[128,1536]{1,0:T(8,128)(2,1)S(1)} %get-tuple-element.642), channel_id=1, source_target_pairs={{64,0},{128,64},{192,128},{256,192},{320,256},{384,320},{448,384},... | collective-permute-start | bytes 1179656 | tf_op jit(solution)/shard_map/while/body/eval_jaxpr/ppermute | solution.py:13
  42.6 11.8 %copy-start.3 = (bf16[2,128,1536]{2,1,0:T(8,128)(2,1)}, bf16[2,128,1536]{2,1,0:T(8,128)(2,1)S(1)}, u32[]{:S(2)}) copy-start(bf16[2,128,1536]{2,1,0:T(8,128)(2,1)S(1)} %bitcast_dynamic-update-slice_fusion.2) | copy-start | bytes 2359300 | tf_op jit(solution)/shard_map/while
  55.7 11.8 %collective-permute-start = (bf16[128,1536]{1,0:T(8,128)(2,1)S(1)}, bf16[128,1536]{1,0:T(8,128)(2,1)S(1)}, u32[]{:S(2)}, u32[]{:S(2)}) collective-permute-start(bf16[128,1536]{1,0:T(8,128)(2,1)S(1)} %get-tuple-element.642), channel_id=1, source_target_pairs={{64,0},{128,64},{192,128},{256,192},{320,256},{384,320},{448,384},... | collective-permute-start | bytes 1179656 | tf_op jit(solution)/shard_map/while/body/eval_jaxpr/ppermute | solution.py:13
  58.3 9.3 %copy-start.3 = (bf16[2,128,1536]{2,1,0:T(8,128)(2,1)}, bf16[2,128,1536]{2,1,0:T(8,128)(2,1)S(1)}, u32[]{:S(2)}) copy-start(bf16[2,128,1536]{2,1,0:T(8,128)(2,1)S(1)} %bitcast_dynamic-update-slice_fusion.2) | copy-start | bytes 2359300 | tf_op jit(solution)/shard_map/while
  68.8 10.8 %collective-permute-start = (bf16[128,1536]{1,0:T(8,128)(2,1)S(1)}, bf16[128,1536]{1,0:T(8,128)(2,1)S(1)}, u32[]{:S(2)}, u32[]{:S(2)}) collective-permute-start(bf16[128,1536]{1,0:T(8,128)(2,1)S(1)} %get-tuple-element.642), channel_id=1, source_target_pairs={{64,0},{128,64},{192,128},{256,192},{320,256},{384,320},{448,384},... | collective-permute-start | bytes 1179656 | tf_op jit(solution)/shard_map/while/body/eval_jaxpr/ppermute | solution.py:13
  71.4 8.2 %copy-start.3 = (bf16[2,128,1536]{2,1,0:T(8,128)(2,1)}, bf16[2,128,1536]{2,1,0:T(8,128)(2,1)S(1)}, u32[]{:S(2)}) copy-start(bf16[2,128,1536]{2,1,0:T(8,128)(2,1)S(1)} %bitcast_dynamic-update-slice_fusion.2) | copy-start | bytes 2359300 | tf_op jit(solution)/shard_map/while
  80.8 11.0 %collective-permute-start = (bf16[128,1536]{1,0:T(8,128)(2,1)S(1)}, bf16[128,1536]{1,0:T(8,128)(2,1)S(1)}, u32[]{:S(2)}, u32[]{:S(2)}) collective-permute-start(bf16[128,1536]{1,0:T(8,128)(2,1)S(1)} %get-tuple-element.642), channel_id=1, source_target_pairs={{64,0},{128,64},{192,128},{256,192},{320,256},{384,320},{448,384},... | collective-permute-start | bytes 1179656 | tf_op jit(solution)/shard_map/while/body/eval_jaxpr/ppermute | solution.py:13
  83.4 8.5 %copy-start.3 = (bf16[2,128,1536]{2,1,0:T(8,128)(2,1)}, bf16[2,128,1536]{2,1,0:T(8,128)(2,1)S(1)}, u32[]{:S(2)}) copy-start(bf16[2,128,1536]{2,1,0:T(8,128)(2,1)S(1)} %bitcast_dynamic-update-slice_fusion.2) | copy-start | bytes 2359300 | tf_op jit(solution)/shard_map/while
  93.1 157.5 %collective-permute-start = (bf16[128,1536]{1,0:T(8,128)(2,1)S(1)}, bf16[128,1536]{1,0:T(8,128)(2,1)S(1)}, u32[]{:S(2)}, u32[]{:S(2)}) collective-permute-start(bf16[128,1536]{1,0:T(8,128)(2,1)S(1)} %get-tuple-element.642), channel_id=1, source_target_pairs={{64,0},{128,64},{192,128},{256,192},{320,256},{384,320},{448,384},... | collective-permute-start | bytes 1179656 | tf_op jit(solution)/shard_map/while/body/eval_jaxpr/ppermute | solution.py:13
  95.7 154.9 %copy-start.3 = (bf16[2,128,1536]{2,1,0:T(8,128)(2,1)}, bf16[2,128,1536]{2,1,0:T(8,128)(2,1)S(1)}, u32[]{:S(2)}) copy-start(bf16[2,128,1536]{2,1,0:T(8,128)(2,1)S(1)} %bitcast_dynamic-update-slice_fusion.2) | copy-start | bytes 2359300 | tf_op jit(solution)/shard_map/while
  252.5 4.7 copy-start.4
  252.5 4.7 copy-start.6
  252.5 4.7 copy-start.8
  252.5 4.7 copy-start.10
  252.5 4.7 copy-start.12
  252.5 4.7 copy-start.14
  252.5 4.7 copy-start.16
  252.5 4.7 copy-start.18
  252.5 4.7 copy-start.20
  252.5 4.7 copy-start.22
  252.6 4.7 copy-start.24
  252.6 4.7 copy-start.26
  252.6 4.7 copy-start.28
  252.6 4.7 copy-start.30
  252.6 4.7 copy-start.32
  252.6 4.7 copy-start.34
  252.6 4.7 copy-start.36
  254.5 13.0 %copy-start.68 = (pred[128]{0:T(512)(128)(4,1)}, pred[128]{0:T(512)(128)(4,1)S(1)}, u32[]{:S(2)}) copy-start(pred[128]{0:T(512)(128)(4,1)S(1)} %iota_compare_fusion) | copy-start | bytes 388 | tf_op jit(solution)/shard_map/while/body/eval_jaxpr/cond
  273.8 11.1 %collective-permute-start = (bf16[128,1536]{1,0:T(8,128)(2,1)S(1)}, bf16[128,1536]{1,0:T(8,128)(2,1)S(1)}, u32[]{:S(2)}, u32[]{:S(2)}) collective-permute-start(bf16[128,1536]{1,0:T(8,128)(2,1)S(1)} %get-tuple-element.642), channel_id=1, source_target_pairs={{64,0},{128,64},{192,128},{256,192},{320,256},{384,320},{448,384},... | collective-permute-start | bytes 1179656 | tf_op jit(solution)/shard_map/while/body/eval_jaxpr/ppermute | solution.py:13
  276.4 8.5 %copy-start.3 = (bf16[2,128,1536]{2,1,0:T(8,128)(2,1)}, bf16[2,128,1536]{2,1,0:T(8,128)(2,1)S(1)}, u32[]{:S(2)}) copy-start(bf16[2,128,1536]{2,1,0:T(8,128)(2,1)S(1)} %bitcast_dynamic-update-slice_fusion.2) | copy-start | bytes 2359300 | tf_op jit(solution)/shard_map/while
  286.7 4.7 copy-start.4
  286.7 4.7 copy-start.6
  286.8 4.7 copy-start.8
  286.8 4.7 copy-start.10
  286.8 4.7 copy-start.12
  286.8 4.7 copy-start.14
  286.8 4.7 copy-start.16
  286.8 4.7 copy-start.18
  286.8 4.7 copy-start.20
  286.8 4.7 copy-start.22
  286.8 4.7 copy-start.24
  286.8 4.7 copy-start.26
  286.9 4.7 copy-start.28
  286.9 4.7 copy-start.30
  286.9 4.7 copy-start.32
  286.9 4.7 copy-start.34
  286.9 4.7 copy-start.36
  288.8 13.0 %copy-start.68 = (pred[128]{0:T(512)(128)(4,1)}, pred[128]{0:T(512)(128)(4,1)S(1)}, u32[]{:S(2)}) copy-start(pred[128]{0:T(512)(128)(4,1)S(1)} %iota_compare_fusion) | copy-start | bytes 388 | tf_op jit(solution)/shard_map/while/body/eval_jaxpr/cond
  291.3 3.8 copy-start.42
  291.3 3.8 copy-start.44
  291.4 3.8 copy-start.46
  291.4 3.8 copy-start.48
  291.4 3.8 copy-start.50
  291.4 3.8 copy-start.52
  291.4 3.8 copy-start.54
  291.4 3.8 copy-start.56
  291.4 3.8 copy-start.58
  308.1 10.2 %collective-permute-start = (bf16[128,1536]{1,0:T(8,128)(2,1)S(1)}, bf16[128,1536]{1,0:T(8,128)(2,1)S(1)}, u32[]{:S(2)}, u32[]{:S(2)}) collective-permute-start(bf16[128,1536]{1,0:T(8,128)(2,1)S(1)} %get-tuple-element.642), channel_id=1, source_target_pairs={{64,0},{128,64},{192,128},{256,192},{320,256},{384,320},{448,384},... | collective-permute-start | bytes 1179656 | tf_op jit(solution)/shard_map/while/body/eval_jaxpr/ppermute | solution.py:13
  310.7 7.6 %copy-start.3 = (bf16[2,128,1536]{2,1,0:T(8,128)(2,1)}, bf16[2,128,1536]{2,1,0:T(8,128)(2,1)S(1)}, u32[]{:S(2)}) copy-start(bf16[2,128,1536]{2,1,0:T(8,128)(2,1)S(1)} %bitcast_dynamic-update-slice_fusion.2) | copy-start | bytes 2359300 | tf_op jit(solution)/shard_map/while
  (126 other events, 205.7 us)
Sparse Core Ops, SparseCore 0:
  319.6 233.0 reduce-scatter.6
where the time goes:
time: 565 us; the launch traced here: 559 us
  waiting for transfers between devices  226 us (40%)
  blocking collectives  216 us (38%)
  local copies, waits for them, and re-layouts  45 us (8%)
  other arithmetic  41.9 us (7%)
  between operations  14.7 us (3%)
  starting transfers between devices  12.8 us (2%)
    unnamed x1, blocking collectives  216 us
    ppermute x9, waiting for transfers between devices, passed_along(): lax.ppermute(value, axis, [(source, source + steps) for source in range(l...  213 us
    unnamed x2, waiting for transfers between devices  13 us
    ppermute x9, starting transfers between devices, passed_along(): lax.ppermute(value, axis, [(source, source + steps) for source in range(l...  12.7 us
  transfers between devices with their start and end apart: 10, of which 10 were waited for; matrix products, arithmetic and copies ran while one was open for 3% of the time, Pallas kernels for 0%

commit v1 on v0

v1 whole, which is shorter than its diff:
```python
import functools
import jax
import jax.numpy as jnp
from jax import lax
from jax.experimental import pallas as pl
from jax.experimental.pallas import tpu as pltpu
from jax.sharding import PartitionSpec as P

KW = 31
HALF = 15
LANES = 128
LEAD = 16
PADDED = 160
EPS = 1e-05
F32 = jnp.float32
BF16 = jnp.bfloat16
VMEM = pl.BlockSpec(memory_space=pltpu.VMEM)
SMEM = pl.BlockSpec(memory_space=pltpu.SMEM)
ANY = pl.BlockSpec(memory_space=pl.ANY)


def columns(block):
    return pl.ds(pl.multiple_of(block * LANES, LANES), LANES)


def row_mean(partial, width):
    return jnp.broadcast_to(jnp.sum(partial, 1, keepdims=True) * (1.0 / width), partial.shape)


def live(length, frames):
    return lax.broadcasted_iota(jnp.int32, (frames, LANES), 0) < length


def clear_margins(pad_ref, frames):
    pad_ref[:, 0:LEAD, :] = jnp.zeros((pad_ref.shape[0], LEAD, LANES), F32)
    tail = PADDED - LEAD - frames
    pad_ref[:, LEAD + frames :, :] = jnp.zeros((pad_ref.shape[0], tail, LANES), F32)


def forward_kernel(len_ref, x_ref, w_ref, s_ref, pad_ref):
    frames, width = x_ref.shape
    blocks = width // LANES
    mask = live(len_ref[0], frames)
    clear_margins(pad_ref, frames)
    zero = jnp.zeros((frames, LANES), F32)

    def convolve(b, total):
        cols = columns(b)
        pad_ref[b, LEAD : LEAD + frames, :] = jnp.where(mask, x_ref[:, cols].astype(F32), 0.0)
        h = zero
        for j in range(KW):
            h = h + w_ref[j : j + 1, cols] * pad_ref[b, LEAD - HALF + j : LEAD - HALF + j + frames, :]
        s_ref[b] = h
        return total + h

    mu = row_mean(lax.fori_loop(0, blocks, convolve, zero), width)

    def square(b, total):
        centred = s_ref[b] - mu
        return total + centred * centred

    recip = lax.rsqrt(row_mean(lax.fori_loop(0, blocks, square, zero), width) + EPS)
    s_ref[2 * blocks] = recip

    def activate(b, carry):
        cols = columns(b)
        normed = (s_ref[b] - mu) * recip
        u = normed * w_ref[KW : KW + 1, cols] + w_ref[KW + 1 : KW + 2, cols]
        sig = jax.nn.sigmoid(u)
        s_ref[b] = normed
        s_ref[blocks + b] = jnp.where(mask, sig * (1.0 + u * (1.0 - sig)), 0.0)
        return carry

    lax.fori_loop(0, blocks, activate, 0)


def forward(length, x, w, limit=16 << 20):
    frames, width = x.shape
    blocks = width // LANES
    return pl.pallas_call(
        forward_kernel,
        out_shape=jax.ShapeDtypeStruct((2 * blocks + 1, frames, LANES), F32),
        in_specs=[SMEM, VMEM, VMEM],
        out_specs=VMEM,
        scratch_shapes=[pltpu.VMEM((blocks, PADDED, LANES), F32)],
        compiler_params=pltpu.CompilerParams(vmem_limit_bytes=limit),
        cost_estimate=pl.CostEstimate(flops=frames * width * 100, bytes_accessed=3 << 20, transcendentals=frames * width),
        name="forward",
    )(length, x, w)


def section(i, mask, dy_ref, s_ref, w_ref, pad_ref, dx_ref, gb_ref, dh_ref):
    frames, width = dy_ref.shape
    blocks = width // LANES
    zero = jnp.zeros((frames, LANES), F32)

    def scale(b, totals):
        first, second = totals
        cols = columns(b)
        normed = s_ref[i, b]
        du = dy_ref[:, cols].astype(F32) * s_ref[i, blocks + b]
        dnorm = du * w_ref[i, KW : KW + 1, cols]
        pad_ref[b, LEAD : LEAD + frames, :] = dnorm
        if gb_ref is not None:
            gb_ref[i, 0:1, cols] = jnp.sum(du * normed, 0, keepdims=True)
            gb_ref[i, 1:2, cols] = jnp.sum(du, 0, keepdims=True)
        return first + dnorm, second + dnorm * normed

    first, second = lax.fori_loop(0, blocks, scale, (zero, zero))
    first, second = row_mean(first, width), row_mean(second, width)

    def convolve(b, carry):
        cols = columns(b)
        dh = s_ref[i, 2 * blocks] * (pad_ref[b, LEAD : LEAD + frames, :] - first - s_ref[i, b] * second)
        pad_ref[b, LEAD : LEAD + frames, :] = dh
        if dh_ref is not None:
            dh_ref[i, b] = dh
        back = dy_ref[:, cols].astype(F32)
        for j in range(KW):
            start = LEAD + HALF - j
            back = back + w_ref[i, j : j + 1, cols] * pad_ref[b, start : start + frames, :]
        dx_ref[:, cols] = jnp.where(mask, back, 0.0).astype(BF16)
        return carry

    lax.fori_loop(0, blocks, convolve, 0)


def phase_kernel(n_dy, last, info_ref, *refs):
    dys = refs[:n_dy]
    s_local, s_other, w_local, w_other = refs[n_dy : n_dy + 4]
    refs = refs[n_dy + 4 :]
    if last:
        own_ref, give_ref, gb_ref, dh_ref = refs[:4]
        dy_ref, first_ref, s_ref, w_ref, pad_ref, sem, dx_ref = refs[4:]
    else:
        dx_ref = refs[0]
        dy_ref, first_ref, s_ref, w_ref, pad_ref, sem = refs[1:]
        gb_ref = dh_ref = None
    length, stage, local_first = info_ref[0], info_ref[1], info_ref[2]
    frames = dy_ref.shape[0]

    def fetch(a, b):
        return [
            pltpu.make_async_copy(a[0], w_ref.at[0], sem.at[1]),
            pltpu.make_async_copy(a[1], s_ref.at[0], sem.at[2]),
            pltpu.make_async_copy(b[0], w_ref.at[1], sem.at[3]),
            pltpu.make_async_copy(b[1], s_ref.at[1], sem.at[4]),
        ]

    chosen = jnp.minimum(stage, n_dy - 1)
    for k in range(n_dy):

        @pl.when(chosen == k)
        def _():
            pltpu.make_async_copy(dys[k], dy_ref, sem.at[0]).start()

    ahead = fetch((w_local, s_local), (w_other, s_other))
    behind = fetch((w_other, s_other), (w_local, s_local))

    @pl.when(local_first == 1)
    def _():
        for copy in ahead:
            copy.start()

    @pl.when(local_first != 1)
    def _():
        for copy in behind:
            copy.start()

    clear_margins(pad_ref, frames)
    mask = live(length, frames)
    pltpu.make_async_copy(dys[0], dy_ref, sem.at[0]).wait()
    ahead[0].wait()
    ahead[1].wait()
    section(0, mask, dy_ref, s_ref, w_ref, pad_ref, first_ref, gb_ref, dh_ref)
    ahead[2].wait()
    ahead[3].wait()
    section(1, mask, first_ref, s_ref, w_ref, pad_ref, dx_ref, gb_ref, dh_ref)
    if last:

        @pl.when(local_first == 1)
        def _():
            own_ref[...] = first_ref[...]
            give_ref[...] = dx_ref[...]

        @pl.when(local_first != 1)
        def _():
            own_ref[...] = dx_ref[...]
            give_ref[...] = first_ref[...]


def phase(info, dys, s_local, s_other, w_local, w_other, last, limit=20 << 20):
    frames, width = dys[0].shape
    blocks = width // LANES
    dx = jax.ShapeDtypeStruct((frames, width), BF16)
    out_shape = [dx]
    scratch = [
        pltpu.VMEM((frames, width), BF16),
        pltpu.VMEM((frames, width), BF16),
        pltpu.VMEM((2,) + s_local.shape, F32),
        pltpu.VMEM((2,) + w_local.shape, F32),
        pltpu.VMEM((blocks, PADDED, LANES), F32),
        pltpu.SemaphoreType.DMA((5,)),
    ]
    if last:
        out_shape = [
            dx,
            dx,
            jax.ShapeDtypeStruct((2, 8, width), F32),
            jax.ShapeDtypeStruct((2, blocks, frames, LANES), F32),
        ]
        scratch.append(pltpu.VMEM((frames, width), BF16))
    return pl.pallas_call(
        functools.partial(phase_kernel, len(dys), last),
        out_shape=out_shape,
        in_specs=[SMEM] + [ANY] * (len(dys) + 4),
        out_specs=[VMEM] * len(out_shape),
        scratch_shapes=scratch,
        compiler_params=pltpu.CompilerParams(vmem_limit_bytes=limit),
        cost_estimate=pl.CostEstimate(flops=frames * width * 160, bytes_accessed=5 << 20, transcendentals=0),
        name="phase_last" if last else "phase",
    )(info, *dys, s_local, s_other, w_local, w_other)


def kernel_grad_kernel(info_ref, x_ref, dh_ref, gb_ref, out_ref, pad_ref):
    frames, width = x_ref.shape
    blocks = width // LANES
    mask = live(info_ref[0], frames)
    clear_margins(pad_ref, frames)
    out_ref[KW + 2 :, :] = jnp.zeros((out_ref.shape[0] - KW - 2, width), out_ref.dtype)

    def correlate(b, carry):
        cols = columns(b)
        pad_ref[b, LEAD : LEAD + frames, :] = jnp.where(mask, x_ref[:, cols].astype(F32), 0.0)
        dh = dh_ref[0, b]
        rows = []
        for j in range(KW):
            product = dh * pad_ref[b, LEAD - HALF + j : LEAD - HALF + j + frames, :]
            rows.append(jnp.sum(product, 0, keepdims=True))
        rows.append(gb_ref[0, 0:1, cols])
        rows.append(gb_ref[0, 1:2, cols])
        out_ref[: KW + 2, cols] = jnp.concatenate(rows, 0).astype(out_ref.dtype)
        return carry

    lax.fori_loop(0, blocks, correlate, 0)


def kernel_grad(info, x, dh, gb, which, dtype, limit=16 << 20):
    frames, width = x.shape
    blocks = width // LANES
    return pl.pallas_call(
        kernel_grad_kernel,
        grid_spec=pltpu.PrefetchScalarGridSpec(
            num_scalar_prefetch=1,
            grid=(1,),
            in_specs=[
                pl.BlockSpec((frames, width), lambda i, s: (0, 0)),
                pl.BlockSpec((1, blocks, frames, LANES), lambda i, s: (s[which], 0, 0, 0)),
                pl.BlockSpec((1, 8, width), lambda i, s: (s[which], 0, 0)),
            ],
            out_specs=pl.BlockSpec((40, width), lambda i, s: (0, 0)),
            scratch_shapes=[pltpu.VMEM((blocks, PADDED, LANES), F32)],
        ),
        out_shape=jax.ShapeDtypeStruct((40, width), dtype),
        compiler_params=pltpu.CompilerParams(vmem_limit_bytes=limit),
        cost_estimate=pl.CostEstimate(flops=frames * width * 62, bytes_accessed=2 << 20, transcendentals=0),
        name="kernel_grad",
    )(info, x, dh, gb)


def pack_kernel(own_ref, other_ref, out_ref, turned_ref):
    rows, width = own_ref.shape
    filler = jnp.zeros((LANES - rows, LANES), F32)

    def turn(b, carry):
        cols = columns(b)
        total = own_ref[:, cols] + other_ref[:, cols].astype(F32)
        turned_ref[columns(b), :] = jnp.concatenate([total, filler], 0).T
        return carry

    lax.fori_loop(0, width // LANES, turn, 0)
    share = width // out_ref.shape[0]

    def gather(d, carry):
        start = pl.multiple_of(d * share, 8)
        packed = turned_ref[pl.ds(start, 8), :]
        for g in range(1, share // 8):
            packed = packed + pltpu.roll(turned_ref[pl.ds(start + 8 * g, 8), :], rows * g, 1)
        out_ref[d] = packed.astype(out_ref.dtype)
        return carry

    lax.fori_loop(0, out_ref.shape[0], gather, 0)


def pack(own, other, members, limit=8 << 20):
    width = own.shape[1]
    return pl.pallas_call(
        pack_kernel,
        out_shape=jax.ShapeDtypeStruct((members, 8, LANES), BF16),
        in_specs=[VMEM, VMEM],
        out_specs=VMEM,
        scratch_shapes=[pltpu.VMEM((width, LANES), F32)],
        compiler_params=pltpu.CompilerParams(vmem_limit_bytes=limit),
        name="pack",
    )(own, other)


def finish_kernel(rows, parts_ref, kernel_ref, gain_ref, bias_ref):
    share = kernel_ref.shape[1]
    total = jnp.sum(parts_ref[...].astype(F32), 0)
    turned = jnp.concatenate([total, jnp.zeros((LANES - 8, LANES), F32)], 0).T
    value = turned[:rows]
    for g in range(1, share // 8):
        value = value + pltpu.roll(turned[rows * g : rows * (g + 1)], 8 * g, 1)
    kernel_ref[...] = value[:KW, :share]
    gain_ref[...] = value[KW : KW + 1, :share]
    bias_ref[...] = value[KW + 1 : KW + 2, :share]


def finish(parts, rows, share, limit=8 << 20):
    return pl.pallas_call(
        functools.partial(finish_kernel, rows),
        out_shape=[
            jax.ShapeDtypeStruct((KW, share), F32),
            jax.ShapeDtypeStruct((1, share), F32),
            jax.ShapeDtypeStruct((1, share), F32),
        ],
        in_specs=[VMEM],
        out_specs=[VMEM, VMEM, VMEM],
        compiler_params=pltpu.CompilerParams(vmem_limit_bytes=limit),
        name="finish",
    )(parts)


def local(saved, out_grad, lengths, kernel, gain, bias):
    sections = lax.axis_size("pipe")
    members = lax.axis_size("dp")
    place = lax.axis_index("pipe")
    upper = place % 2
    item = 1 - upper
    stages = sections // 2
    stage = stages - 1 - place // 2
    swap = [(p, p ^ 1) for p in range(sections)]
    x_both = saved[0, :, 0]
    x_give = lax.dynamic_index_in_dim(x_both, 1 - item, 0, keepdims=False)
    x_local = lax.dynamic_index_in_dim(x_both, item, 0, keepdims=False)
    w_local = jnp.concatenate([kernel[0].astype(F32), gain, bias], 0)
    w_other = lax.ppermute(w_local, "pipe", swap)
    x_other = lax.ppermute(x_give, "pipe", swap)
    dys = [lax.dynamic_index_in_dim(out_grad[:, 0], item, 0, keepdims=False)]
    length = lax.dynamic_index_in_dim(lengths[:, 0], item, 0, keepdims=False)
    info = jnp.stack([length, stage, upper, 1 - upper, upper]).astype(jnp.int32)
    s_local = forward(info, x_local, w_local)
    s_other = forward(info, x_other, w_other)
    for k in range(stages - 1):
        (dx,) = phase(info, dys, s_local, s_other, w_local, w_other, False)
        top = sections - 1 - 2 * k
        dys.append(lax.ppermute(dx, "pipe", [(top, top - 2), (top - 1, top - 3)]))
    own, give, gb, dh = phase(info, dys, s_local, s_other, w_local, w_other, True)
    kg_give = kernel_grad(info, x_other, dh, gb, 4, BF16)
    kg_other = lax.ppermute(kg_give, "pipe", swap)
    dx_other = lax.ppermute(give, "pipe", swap)
    kg_own = kernel_grad(info, x_local, dh, gb, 3, F32)
    packed = pack(kg_own, kg_other, members)
    parts = lax.all_to_all(packed, "dp", 0, 0, tiled=True)
    kernel_part, gain_part, bias_part = finish(parts, kg_own.shape[0], kernel.shape[2] // members)
    grads = jnp.where(item == 0, jnp.stack([own, dx_other]), jnp.stack([dx_other, own]))
    return (grads[None, :, None], kernel_part[None], gain_part, bias_part)


def solution(mesh):
    return jax.shard_map(
        local,
        mesh=mesh,
        in_specs=(
            P("pipe", None, "dp", None, None),
            P(None, "dp", None, None),
            P(None, "dp"),
            P("pipe", None, None),
            P("pipe", None),
            P("pipe", None),
        ),
        out_specs=(
            P("pipe", None, "dp", None, None),
            P("pipe", None, "dp"),
            P("pipe", "dp"),
            P("pipe", "dp"),
        ),
        check_vma=False,
    )
```

time: 565 us -> 142 us (0.25)
  blocking collectives: 216 us -> 0 us
  waiting for transfers between devices: 226 us -> 53.5 us
  Pallas kernels: 0 us -> 46.2 us
  local copies, waits for them, and re-layouts: 45 us -> 3.3 us
  other arithmetic: 41.9 us -> 1.05 us
  starting transfers between devices: 12.8 us -> 37 us
  between operations: 14.7 us -> 0.93 us
    unnamed x1 -> x0, blocking collectives: 216 us -> none
    ppermute x9 -> x7, waiting for transfers between devices: 213 us -> 37.4 us  [the longest x3 29.9 us: local(): dys.append(lax.ppermute(dx, 'pipe', [(top, top - 2), (top - 1, top - 3)]))]
    pallas_call x0 -> x10, Pallas kernels: none -> 46.2 us  [the longest x4 27.2 us: phase(): pl.pallas_call(functools.partial(phase_kernel, len(dys), last), out_shape...]
    all_to_all x0 -> x1, starting transfers between devices: none -> 19.9 us  [local(): parts = lax.all_to_all(packed, 'dp', 0, 0, tiled=True)]
    reduce_sum x10 -> x0, other arithmetic: 19.6 us -> none  [the longest x4 8.01 us: backward_frames(): jnp.sum(dh * padded[j:j + frames], 0)]
    all_to_all x0 -> x1, waiting for transfers between devices: none -> 16 us  [local(): parts = lax.all_to_all(packed, 'dp', 0, 0, tiled=True)]
    unnamed x2 -> x0, waiting for transfers between devices: 13 us -> none
    while x109 -> x0, local copies, waits for them, and re-layouts: 11.2 us -> none
  transfers between devices with their start and end apart: 10 -> 8, of which waited for: 10 -> 4; matrix products, arithmetic and copies ran while one was open for 3% -> 2% of each run, Pallas kernels for 0% -> 11%
where the time goes in v1:
time: 142 us
  waiting for transfers between devices  53.5 us (38%)
  Pallas kernels  46.2 us (33%)
  starting transfers between devices  37 us (26%)
  local copies, waits for them, and re-layouts  3.3 us (2%)
    ppermute x3, waiting for transfers between devices, local(): dys.append(lax.ppermute(dx, 'pipe', [(top, top - 2), (top - 1, top - 3)]))  29.9 us
    pallas_call x4, Pallas kernels, phase(): pl.pallas_call(functools.partial(phase_kernel, len(dys), last), out_shape...  27.2 us
    all_to_all x1, starting transfers between devices, local(): parts = lax.all_to_all(packed, 'dp', 0, 0, tiled=True)  19.9 us
    all_to_all x1, waiting for transfers between devices, local(): parts = lax.all_to_all(packed, 'dp', 0, 0, tiled=True)  16 us
    pallas_call x1, Pallas kernels, pack(): pl.pallas_call(pack_kernel, out_shape=jax.ShapeDtypeStruct((members, 8, L...  6.54 us
    pallas_call x2, Pallas kernels, forward(): pl.pallas_call(forward_kernel, out_shape=jax.ShapeDtypeStruct((2 * blocks...  6.1 us
    ppermute x1, starting transfers between devices, local(): x_other = lax.ppermute(x_give, 'pipe', swap)  5.64 us
    pallas_call x2, Pallas kernels, kernel_grad(): pl.pallas_call(kernel_grad_kernel, grid_spec=pltpu.PrefetchScalarGridSpec...  5.63 us
  transfers between devices with their start and end apart: 8, of which 4 were waited for; matrix products, arithmetic and copies ran while one was open for 2% of the time, Pallas kernels for 11%

profile of v1, /device:TPU:1, one launch (start us, length us, event | category | flops | bytes accessed | tf_op | source)
XLA Modules:
  0.0 141.9 jit_solution(2627426794045783857)
XLA Ops:
  0.6 0.0 copy-start
  0.6 0.0 copy-start.1
  0.7 0.0 copy-start.2
  0.7 0.0 copy-start.3
  0.7 0.0 copy-start.4
  0.7 1.2 dynamic-slice_bitcast_fusion
  2.0 5.6 %collective-permute-start = (bf16[128,1536]{1,0:T(8,128)(2,1)S(1)}, bf16[128,1536]{1,0:T(8,128)(2,1)S(1)}, u32[]{:S(2)}, u32[]{:S(2)}) collective-permute-start(bf16[128,1536]{1,0:T(8,128)(2,1)S(1)} %get-tuple-element.22), channel_id=1, source_target_pairs={{0,64},{64,0},{128,192},{192,128},{256,320},{320,256},{384,448},{4... | collective-permute-start | bytes 1179656 | tf_op jit(solution)/shard_map/ppermute | solution.py:349
  7.6 0.0 copy-done.1
  7.6 0.0 copy-done.2
  7.7 0.0 copy-done.3
  7.7 1.9 %collective-permute-start.1 = (f32[33,1536]{1,0:T(8,128)S(1)}, f32[33,1536]{1,0:T(8,128)S(1)}, u32[]{:S(2)}, u32[]{:S(2)}) collective-permute-start(f32[33,1536]{1,0:T(8,128)S(1)} %pad_maximum_fusion.w_ref.refs_3_.refs_4_.refs_5_.refs_6_), channel_id=1, source_target_pairs={{0,64},{64,0},{128,192},{192,128},{256,320},{320,256},{384,448},{4... | collective-permute-start | bytes 608264 | tf_op jit(solution)/shard_map/ppermute | solution.py:348
  9.6 0.0 copy-done.4
  9.6 0.6 constant_dynamic-slice_fusion
  10.2 0.7 stack.31.len_ref.info_ref
  11.0 3.1 %forward.2.refs_1_.refs_2_.refs_3_.refs_4_ = f32[25,128,128]{2,1,0:T(8,128)S(1)} custom-call(s32[5]{0:T(128)S(1)} %stack.31.len_ref.info_ref, bf16[128,1536]{1,0:T(8,128)(2,1)S(1)} %get-tuple-element.23.x_ref, f32[33,1536]{1,0:T(8,128)S(1)} %pad_maximum_fusion.w_ref.refs_3_.refs_4_.refs_5_.refs_6_), custom_call_target="tpu_custom_call" | custom-call | flops 19660800 | bytes 3145728 | tf_op jit(solution)/shard_map/forward/pallas_call | solution.py:80
  14.0 0.0 copy-done
  14.1 4.4 %collective-permute-done.1.w_ref.refs_4_.refs_5_.refs_6_.refs_7_ = f32[33,1536]{1,0:T(8,128)S(1)} collective-permute-done((f32[33,1536]{1,0:T(8,128)S(1)}, f32[33,1536]{1,0:T(8,128)S(1)}, u32[]{:S(2)}, u32[]{:S(2)}) %collective-permute-start.1) | collective-permute-done | bytes 202784 | tf_op jit(solution)/shard_map/ppermute | solution.py:348
  18.5 0.0 collective-permute-done.x_ref
  18.5 3.1 %forward.3.refs_2_.refs_3_.refs_4_.refs_5_ = f32[25,128,128]{2,1,0:T(8,128)S(1)} custom-call(s32[5]{0:T(128)S(1)} %stack.31.len_ref.info_ref, bf16[128,1536]{1,0:T(8,128)(2,1)S(1)} %collective-permute-done.x_ref, f32[33,1536]{1,0:T(8,128)S(1)} %collective-permute-done.1.w_ref.refs_4_.refs_5_.refs_6_.refs_7_), custom_call_target="tpu_custom_call" | custom-call | flops 19660800 | bytes 3145728 | tf_op jit(solution)/shard_map/forward/pallas_call | solution.py:80
  21.5 6.7 %phase.3 = bf16[128,1536]{1,0:T(8,128)(2,1)S(1)} custom-call(s32[5]{0:T(128)S(1)} %stack.31.len_ref.info_ref, bf16[128,1536]{1,0:T(8,128)(2,1)S(1)} %dynamic-slice_bitcast_fusion.2.refs_0_, f32[25,128,128]{2,1,0:T(8,128)S(1)} %forward.2.refs_1_.refs_2_.refs_3_.refs_4_, f32[25,128,128]{2,1,0:T(8,128)S(1)} %forward.3.refs_2_.refs_3_.refs_4_.refs_5_, ...), custom_call_target="tpu_custom_call" | custom-call | flops 31457280 | bytes 5242880 | tf_op jit(solution)/shard_map/phase/pallas_call | solution.py:213
  28.2 0.7 collective-permute-start.2
  28.9 0.0 collective-permute-done.2.refs_1_
  29.0 6.7 %phase.4 = bf16[128,1536]{1,0:T(8,128)(2,1)S(1)} custom-call(s32[5]{0:T(128)S(1)} %stack.31.len_ref.info_ref, bf16[128,1536]{1,0:T(8,128)(2,1)S(1)} %dynamic-slice_bitcast_fusion.2.refs_0_, bf16[128,1536]{1,0:T(8,128)(2,1)S(1)} %collective-permute-done.2.refs_1_, f32[25,128,128]{2,1,0:T(8,128)S(1)} %forward.2.refs_1_.refs_2_.refs_3_.refs_4_, ...), custom_call_target="tpu_custom_call" | custom-call | flops 31457280 | bytes 5242880 | tf_op jit(solution)/shard_map/phase/pallas_call | solution.py:213
  35.7 0.7 collective-permute-start.3
  36.4 0.0 collective-permute-done.3.refs_2_
  36.4 6.7 %phase.5 = bf16[128,1536]{1,0:T(8,128)(2,1)S(1)} custom-call(s32[5]{0:T(128)S(1)} %stack.31.len_ref.info_ref, bf16[128,1536]{1,0:T(8,128)(2,1)S(1)} %dynamic-slice_bitcast_fusion.2.refs_0_, bf16[128,1536]{1,0:T(8,128)(2,1)S(1)} %collective-permute-done.2.refs_1_, bf16[128,1536]{1,0:T(8,128)(2,1)S(1)} %collective-permute-done.3.refs_2_, ...), custom_call_target="tpu_custom_call" | custom-call | flops 31457280 | bytes 5242880 | tf_op jit(solution)/shard_map/phase/pallas_call | solution.py:213
  43.1 1.3 collective-permute-start.4
  44.4 29.9 %collective-permute-done.4.refs_3_ = bf16[128,1536]{1,0:T(8,128)(2,1)S(1)} collective-permute-done((bf16[128,1536]{1,0:T(8,128)(2,1)S(1)}, bf16[128,1536]{1,0:T(8,128)(2,1)S(1)}, u32[]{:S(2)}, u32[]{:S(2)}) %collective-permute-start.4) | collective-permute-done | bytes 393248 | tf_op jit(solution)/shard_map/ppermute | solution.py:358
  74.3 7.1 %phase_last.1 = (bf16[128,1536]{1,0:T(8,128)(2,1)S(1)}, bf16[128,1536]{1,0:T(8,128)(2,1)S(1)}, f32[2,8,1536]{2,1,0:T(8,128)S(1)}, f32[2,12,128,128]{3,2,1,0:T(8,128)S(1)}) custom-call(s32[5]{0:T(128)S(1)} %stack.31.len_ref.info_ref, bf16[128,1536]{1,0:T(8,128)(2,1)S(1)} %dynamic-slice_bitcast_fusion.2.refs_0_, ...), custom_call_target="tpu_custom_call" | custom-call | flops 31457280 | bytes 5242880 | tf_op jit(solution)/shard_map/phase_last/pallas_call | solution.py:213
  81.4 4.8 %collective-permute-start.5 = (bf16[128,1536]{1,0:T(8,128)(2,1)S(1)}, bf16[128,1536]{1,0:T(8,128)(2,1)S(1)}, u32[]{:S(2)}, u32[]{:S(2)}) collective-permute-start(bf16[128,1536]{1,0:T(8,128)(2,1)S(1)} %get-tuple-element.12), channel_id=1, source_target_pairs={{0,64},{64,0},{128,192},{192,128},{256,320},{320,256},{384,448},{4... | collective-permute-start | bytes 1179656 | tf_op jit(solution)/shard_map/ppermute | solution.py:362
  86.2 2.8 %kernel_grad.3 = bf16[40,1536]{1,0:T(8,128)(2,1)S(1)} custom-call(s32[5]{0:T(128)S(1)} %stack.31.len_ref.info_ref, bf16[128,1536]{1,0:T(8,128)(2,1)S(1)} %collective-permute-done.x_ref, f32[2,12,128,128]{3,2,1,0:T(8,128)S(1)} %get-tuple-element.13.dh_ref, f32[2,8,1536]{2,1,0:T(8,128)S(1)} %get-tuple-element.14.gb_ref), custom_call_target="tpu_custom_call" | custom-call | flops 12189696 | bytes 2097152 | tf_op jit(solution)/shard_map/kernel_grad/pallas_call | solution.py:251
  89.0 2.0 %collective-permute-start.6 = (bf16[40,1536]{1,0:T(8,128)(2,1)S(1)}, bf16[40,1536]{1,0:T(8,128)(2,1)S(1)}, u32[]{:S(2)}, u32[]{:S(2)}) collective-permute-start(bf16[40,1536]{1,0:T(8,128)(2,1)S(1)} %kernel_grad.3), channel_id=1, source_target_pairs={{0,64},{64,0},{128,192},{192,128},{256,320},{320,256},{384,448},{4... | collective-permute-start | bytes 368648 | tf_op jit(solution)/shard_map/ppermute | solution.py:361
  91.0 2.8 %kernel_grad.2.own_ref = f32[40,1536]{1,0:T(8,128)S(1)} custom-call(s32[5]{0:T(128)S(1)} %stack.31.len_ref.info_ref, bf16[128,1536]{1,0:T(8,128)(2,1)S(1)} %get-tuple-element.23.x_ref, f32[2,12,128,128]{3,2,1,0:T(8,128)S(1)} %get-tuple-element.13.dh_ref, f32[2,8,1536]{2,1,0:T(8,128)S(1)} %get-tuple-element.14.gb_ref), custom_call_target="tpu_custom_call" | custom-call | flops 12189696 | bytes 2097152 | tf_op jit(solution)/shard_map/kernel_grad/pallas_call | solution.py:251
  93.8 3.1 %collective-permute-done.6.other_ref = bf16[40,1536]{1,0:T(8,128)(2,1)S(1)} collective-permute-done((bf16[40,1536]{1,0:T(8,128)(2,1)S(1)}, bf16[40,1536]{1,0:T(8,128)(2,1)S(1)}, u32[]{:S(2)}, u32[]{:S(2)}) %collective-permute-start.6) | collective-permute-done | bytes 122912 | tf_op jit(solution)/shard_map/ppermute | solution.py:361
  96.9 6.5 %pack.1 = bf16[64,8,128]{2,1,0:T(8,128)(2,1)} custom-call(f32[40,1536]{1,0:T(8,128)S(1)} %kernel_grad.2.own_ref, bf16[40,1536]{1,0:T(8,128)(2,1)S(1)} %collective-permute-done.6.other_ref), custom_call_target="tpu_custom_call" | custom-call | tf_op jit(solution)/shard_map/pack/pallas_call | solution.py:297
  103.5 19.9 %all-to-all-start = ((bf16[64,8,128]{2,1,0:T(8,128)(2,1)}), bf16[64,8,128]{2,1,0:T(8,128)(2,1)S(1)}, u32[]{:S(2)}, u32[]{:S(2)}) async-start(bf16[64,8,128]{2,1,0:T(8,128)(2,1)} %pack.1), calls=%async_computation | async-start | bytes 262144 | tf_op jit(solution)/shard_map/all_to_all | solution.py:365
  123.4 0.0 collective-permute-done.5
  123.4 1.0 maximum_select_fusion
  124.4 16.0 %all-to-all-done.parts_ref = bf16[64,8,128]{2,1,0:T(8,128)(2,1)S(1)} async-done(((bf16[64,8,128]{2,1,0:T(8,128)(2,1)}), bf16[64,8,128]{2,1,0:T(8,128)(2,1)S(1)}, u32[]{:S(2)}, u32[]{:S(2)}) %all-to-all-start) | async-done | bytes 131104 | tf_op jit(solution)/shard_map/all_to_all | solution.py:365
  140.5 0.7 finish.1
  141.2 0.7 copy.10
  (3 shorter events, 0.1 us)
Async XLA Ops:
  0.6 13.4 %copy-start = (bf16[2,1,128,1536]{3,2,1,0:T(8,128)(2,1)S(1)}, bf16[2,1,128,1536]{3,2,1,0:T(8,128)(2,1)}, u32[]{:S(2)}) copy-start(bf16[2,1,128,1536]{3,2,1,0:T(8,128)(2,1)} %param.7) | copy-start | bytes 2359300
  0.6 7.0 %copy-start.1 = (bf16[1,31,1536]{2,1,0:T(8,128)(2,1)S(1)}, bf16[1,31,1536]{2,1,0:T(8,128)(2,1)}, u32[]{:S(2)}) copy-start(bf16[1,31,1536]{2,1,0:T(8,128)(2,1)} %param.9) | copy-start | bytes 285700
  0.7 7.0 %copy-start.2 = (f32[1,1536]{1,0:T(1,128)S(1)}, f32[1,1536]{1,0:T(1,128)}, u32[]{:S(2)}) copy-start(f32[1,1536]{1,0:T(1,128)} %param.11) | copy-start | bytes 18436
  0.7 7.0 %copy-start.3 = (f32[1,1536]{1,0:T(1,128)S(1)}, f32[1,1536]{1,0:T(1,128)}, u32[]{:S(2)}) copy-start(f32[1,1536]{1,0:T(1,128)} %param.10) | copy-start | bytes 18436
  0.7 9.0 %copy-start.4 = (s32[2,1]{0,1:T(1,128)S(1)}, s32[2,1]{0,1:T(1,128)}, u32[]{:S(2)}) copy-start(s32[2,1]{0,1:T(1,128)} %param.8) | copy-start | bytes 28
  2.0 16.5 %collective-permute-start = (bf16[128,1536]{1,0:T(8,128)(2,1)S(1)}, bf16[128,1536]{1,0:T(8,128)(2,1)S(1)}, u32[]{:S(2)}, u32[]{:S(2)}) collective-permute-start(bf16[128,1536]{1,0:T(8,128)(2,1)S(1)} %get-tuple-element.22), channel_id=1, source_target_pairs={{0,64},{64,0},{128,192},{192,128},{256,320},{320,256},{384,448},{4... | collective-permute-start | bytes 1179656 | tf_op jit(solution)/shard_map/ppermute | solution.py:349
  7.7 10.8 %collective-permute-start.1 = (f32[33,1536]{1,0:T(8,128)S(1)}, f32[33,1536]{1,0:T(8,128)S(1)}, u32[]{:S(2)}, u32[]{:S(2)}) collective-permute-start(f32[33,1536]{1,0:T(8,128)S(1)} %pad_maximum_fusion.w_ref.refs_3_.refs_4_.refs_5_.refs_6_), channel_id=1, source_target_pairs={{0,64},{64,0},{128,192},{192,128},{256,320},{320,256},{384,448},{4... | collective-permute-start | bytes 608264 | tf_op jit(solution)/shard_map/ppermute | solution.py:348
  28.2 0.7 collective-permute-start.2
  35.7 0.7 collective-permute-start.3
  43.1 31.2 %collective-permute-start.4 = (bf16[128,1536]{1,0:T(8,128)(2,1)S(1)}, bf16[128,1536]{1,0:T(8,128)(2,1)S(1)}, u32[]{:S(2)}, u32[]{:S(2)}) collective-permute-start(bf16[128,1536]{1,0:T(8,128)(2,1)S(1)} %phase.5), channel_id=1, source_target_pairs={{192,64},{128,0},{193,65},{129,1},{194,66},{130,2},{195,67},{131,3... | collective-permute-start | bytes 1179656 | tf_op jit(solution)/shard_map/ppermute | solution.py:358
  81.4 42.0 %collective-permute-start.5 = (bf16[128,1536]{1,0:T(8,128)(2,1)S(1)}, bf16[128,1536]{1,0:T(8,128)(2,1)S(1)}, u32[]{:S(2)}, u32[]{:S(2)}) collective-permute-start(bf16[128,1536]{1,0:T(8,128)(2,1)S(1)} %get-tuple-element.12), channel_id=1, source_target_pairs={{0,64},{64,0},{128,192},{192,128},{256,320},{320,256},{384,448},{4... | collective-permute-start | bytes 1179656 | tf_op jit(solution)/shard_map/ppermute | solution.py:362
  89.0 7.9 %collective-permute-start.6 = (bf16[40,1536]{1,0:T(8,128)(2,1)S(1)}, bf16[40,1536]{1,0:T(8,128)(2,1)S(1)}, u32[]{:S(2)}, u32[]{:S(2)}) collective-permute-start(bf16[40,1536]{1,0:T(8,128)(2,1)S(1)} %kernel_grad.3), channel_id=1, source_target_pairs={{0,64},{64,0},{128,192},{192,128},{256,320},{320,256},{384,448},{4... | collective-permute-start | bytes 368648 | tf_op jit(solution)/shard_map/ppermute | solution.py:361
  103.5 37.0 %all-to-all-start = ((bf16[64,8,128]{2,1,0:T(8,128)(2,1)}), bf16[64,8,128]{2,1,0:T(8,128)(2,1)S(1)}, u32[]{:S(2)}, u32[]{:S(2)}) async-start(bf16[64,8,128]{2,1,0:T(8,128)(2,1)} %pack.1), calls=%async_computation | async-start | bytes 262144 | tf_op jit(solution)/shard_map/all_to_all | solution.py:365

commit v2 on v1

--- a/solution.py
+++ b/solution.py
@@ -6,12 +6,14 @@
 from jax.experimental.pallas import tpu as pltpu
 from jax.sharding import PartitionSpec as P
 
+
 KW = 31
 HALF = 15
 LANES = 128
 LEAD = 16
 PADDED = 160
 EPS = 1e-05
+ROWS = 40
 F32 = jnp.float32
 BF16 = jnp.bfloat16
 VMEM = pl.BlockSpec(memory_space=pltpu.VMEM)
@@ -222,34 +224,42 @@
     )(info, *dys, s_local, s_other, w_local, w_other)
 
 
-def kernel_grad_kernel(info_ref, x_ref, dh_ref, gb_ref, out_ref, pad_ref):
+def kernel_grad_kernel(rows, info_ref, x_ref, dh_ref, gb_ref, out_ref, pad_ref, turned_ref):
     frames, width = x_ref.shape
     blocks = width // LANES
+    members = out_ref.shape[0]
+    share = width // members
     mask = live(info_ref[0], frames)
     clear_margins(pad_ref, frames)
-    out_ref[KW + 2 :, :] = jnp.zeros((out_ref.shape[0] - KW - 2, width), out_ref.dtype)
+    filler = jnp.zeros((LANES - KW - 2, LANES), F32)
 
     def correlate(b, carry):
         cols = columns(b)
         pad_ref[b, LEAD : LEAD + frames, :] = jnp.where(mask, x_ref[:, cols].astype(F32), 0.0)
         dh = dh_ref[0, b]
-        rows = []
+        sums = []
         for j in range(KW):
             product = dh * pad_ref[b, LEAD - HALF + j : LEAD - HALF + j + frames, :]
-            rows.append(jnp.sum(product, 0, keepdims=True))
-        rows.append(gb_ref[0, 0:1, cols])
-        rows.append(gb_ref[0, 1:2, cols])
-        out_ref[: KW + 2, cols] = jnp.concatenate(rows, 0).astype(out_ref.dtype)
+            sums.append(jnp.sum(product, 0, keepdims=True))
+        sums.append(gb_ref[0, 0:1, cols])
+        sums.append(gb_ref[0, 1:2, cols])
+        turned_ref[cols, :] = jnp.concatenate(sums + [filler], 0).T
         return carry
 
     lax.fori_loop(0, blocks, correlate, 0)
-
-
-def kernel_grad(info, x, dh, gb, which, dtype, limit=16 << 20):
+    for d in range(members):
+        start = d * share
+        packed = turned_ref[start : start + 8, :]
+        for g in range(1, share // 8):
+            packed = packed + pltpu.roll(turned_ref[start + 8 * g : start + 8 * g + 8, :], rows * g, 1)
+        out_ref[d] = packed.astype(out_ref.dtype)
+
+
+def kernel_grad(info, x, dh, gb, which, members, dtype, limit=16 << 20):
     frames, width = x.shape
     blocks = width // LANES
     return pl.pallas_call(
-        kernel_grad_kernel,
+        functools.partial(kernel_grad_kernel, ROWS),
         grid_spec=pltpu.PrefetchScalarGridSpec(
             num_scalar_prefetch=1,
             grid=(1,),
@@ -258,70 +268,32 @@
                 pl.BlockSpec((1, blocks, frames, LANES), lambda i, s: (s[which], 0, 0, 0)),
                 pl.BlockSpec((1, 8, width), lambda i, s: (s[which], 0, 0)),
             ],
-            out_specs=pl.BlockSpec((40, width), lambda i, s: (0, 0)),
-            scratch_shapes=[pltpu.VMEM((blocks, PADDED, LANES), F32)],
+            out_specs=pl.BlockSpec((members, 8, LANES), lambda i, s: (0, 0, 0)),
+            scratch_shapes=[pltpu.VMEM((blocks, PADDED, LANES), F32), pltpu.VMEM((width, LANES), F32)],
         ),
-        out_shape=jax.ShapeDtypeStruct((40, width), dtype),
+        out_shape=jax.ShapeDtypeStruct((members, 8, LANES), dtype),
         compiler_params=pltpu.CompilerParams(vmem_limit_bytes=limit),
         cost_estimate=pl.CostEstimate(flops=frames * width * 62, bytes_accessed=2 << 20, transcendentals=0),
         name="kernel_grad",
     )(info, x, dh, gb)
 
 
-def pack_kernel(own_ref, other_ref, out_ref, turned_ref):
-    rows, width = own_ref.shape
-    filler = jnp.zeros((LANES - rows, LANES), F32)
-
-    def turn(b, carry):
-        cols = columns(b)
-        total = own_ref[:, cols] + other_ref[:, cols].astype(F32)
-        turned_ref[columns(b), :] = jnp.concatenate([total, filler], 0).T
-        return carry
-
-    lax.fori_loop(0, width // LANES, turn, 0)
-    share = width // out_ref.shape[0]
-
-    def gather(d, carry):
-        start = pl.multiple_of(d * share, 8)
-        packed = turned_ref[pl.ds(start, 8), :]
-        for g in range(1, share // 8):
-            packed = packed + pltpu.roll(turned_ref[pl.ds(start + 8 * g, 8), :], rows * g, 1)
-        out_ref[d] = packed.astype(out_ref.dtype)
-        return carry
-
-    lax.fori_loop(0, out_ref.shape[0], gather, 0)
-
-
-def pack(own, other, members, limit=8 << 20):
-    width = own.shape[1]
+def finish_kernel(rows, parts_ref, kernel_ref, gain_ref, bias_ref):
+    share = kernel_ref.shape[0]
+    total = jnp.sum(parts_ref[...].astype(F32), 0)
+    pieces = [total] + [pltpu.roll(total, LANES - rows * g, 1) for g in range(1, share // 8)]
+    value = jnp.concatenate(pieces + [jnp.zeros((LANES - share, LANES), F32)], 0)
+    kernel_ref[...] = value[:share, :KW]
+    turned = value.T
+    gain_ref[...] = turned[KW : KW + 1, :share]
+    bias_ref[...] = turned[KW + 1 : KW + 2, :share]
+
+
+def finish(parts, share, limit=8 << 20):
     return pl.pallas_call(
-        pack_kernel,
-        out_shape=jax.ShapeDtypeStruct((members, 8, LANES), BF16),
-        in_specs=[VMEM, VMEM],
-        out_specs=VMEM,
-        scratch_shapes=[pltpu.VMEM((width, LANES), F32)],
-        compiler_params=pltpu.CompilerParams(vmem_limit_bytes=limit),
-        name="pack",
-    )(own, other)
-
-
-def finish_kernel(rows, parts_ref, kernel_ref, gain_ref, bias_ref):
-    share = kernel_ref.shape[1]
-    total = jnp.sum(parts_ref[...].astype(F32), 0)
-    turned = jnp.concatenate([total, jnp.zeros((LANES - 8, LANES), F32)], 0).T
-    value = turned[:rows]
-    for g in range(1, share // 8):
-        value = value + pltpu.roll(turned[rows * g : rows * (g + 1)], 8 * g, 1)
-    kernel_ref[...] = value[:KW, :share]
-    gain_ref[...] = value[KW : KW + 1, :share]
-    bias_ref[...] = value[KW + 1 : KW + 2, :share]
-
-
-def finish(parts, rows, share, limit=8 << 20):
-    return pl.pallas_call(
-        functools.partial(finish_kernel, rows),
+        functools.partial(finish_kernel, ROWS),
         out_shape=[
-            jax.ShapeDtypeStruct((KW, share), F32),
+            jax.ShapeDtypeStruct((share, KW), F32),
             jax.ShapeDtypeStruct((1, share), F32),
             jax.ShapeDtypeStruct((1, share), F32),
         ],
@@ -357,15 +329,15 @@
         top = sections - 1 - 2 * k
         dys.append(lax.ppermute(dx, "pipe", [(top, top - 2), (top - 1, top - 3)]))
     own, give, gb, dh = phase(info, dys, s_local, s_other, w_local, w_other, True)
-    kg_give = kernel_grad(info, x_other, dh, gb, 4, BF16)
+    kg_give = kernel_grad(info, x_other, dh, gb, 4, members, BF16)
     kg_other = lax.ppermute(kg_give, "pipe", swap)
+    kg_own = kernel_grad(info, x_local, dh, gb, 3, members, F32)
+    packed = (kg_own + kg_other.astype(F32)).astype(BF16)
+    parts = lax.all_to_all(packed, "dp", 0, 0, tiled=True)
     dx_other = lax.ppermute(give, "pipe", swap)
-    kg_own = kernel_grad(info, x_local, dh, gb, 3, F32)
-    packed = pack(kg_own, kg_other, members)
-    parts = lax.all_to_all(packed, "dp", 0, 0, tiled=True)
-    kernel_part, gain_part, bias_part = finish(parts, kg_own.shape[0], kernel.shape[2] // members)
+    kernel_part, gain_part, bias_part = finish(parts, kernel.shape[2] // members)
     grads = jnp.where(item == 0, jnp.stack([own, dx_other]), jnp.stack([dx_other, own]))
-    return (grads[None, :, None], kernel_part[None], gain_part, bias_part)
+    return (grads[None, :, None], kernel_part.T[None], gain_part, bias_part)
 
 
 def solution(mesh):

time: 142 us -> 136 us (0.958)
  Pallas kernels: 46.2 us -> 42.4 us
  waiting for transfers between devices: 53.5 us -> 50.4 us
    pallas_call x4 -> x3, Pallas kernels: 12.9 us -> 9.11 us  [the longest x2 8.37 us: kernel_grad(): pl.pallas_call(functools.partial(kernel_grad_kernel, ROWS), grid_spec=plt...]
    ppermute x1, waiting for transfers between devices: 3.11 us -> 0.01 us  [local(): kg_other = lax.ppermute(kg_give, 'pipe', swap)]
    ppermute x1, starting transfers between devices: 4.82 us -> 1.96 us  [local(): dx_other = lax.ppermute(give, 'pipe', swap)]
    ppermute x1, starting transfers between devices: 1.96 us -> 4.82 us  [local(): kg_other = lax.ppermute(kg_give, 'pipe', swap)]
  transfers between devices with their start and end apart: 8 -> 8, of which waited for: 4 -> 3; matrix products, arithmetic and copies ran while one was open for 2% -> 2% of each run, Pallas kernels for 11% -> 5%
where the time goes in v2:
time: 136 us
  waiting for transfers between devices  50.4 us (37%)
  Pallas kernels  42.4 us (31%)
  starting transfers between devices  37.8 us (28%)
  local copies, waits for them, and re-layouts  2.62 us (2%)
  other arithmetic  1.74 us (1%)
    ppermute x3, waiting for transfers between devices, local(): dys.append(lax.ppermute(dx, 'pipe', [(top, top - 2), (top - 1, top - 3)]))  29.9 us
    pallas_call x4, Pallas kernels, phase(): pl.pallas_call(functools.partial(phase_kernel, len(dys), last), out_shape...  27.2 us
    all_to_all x1, starting transfers between devices, local(): parts = lax.all_to_all(packed, 'dp', 0, 0, tiled=True)  20.8 us
    all_to_all x1, waiting for transfers between devices, local(): parts = lax.all_to_all(packed, 'dp', 0, 0, tiled=True)  16.1 us
    pallas_call x2, Pallas kernels, kernel_grad(): pl.pallas_call(functools.partial(kernel_grad_kernel, ROWS), grid_spec=plt...  8.37 us
    pallas_call x2, Pallas kernels, forward(): pl.pallas_call(forward_kernel, out_shape=jax.ShapeDtypeStruct((2 * blocks...  6.1 us
    ppermute x1, starting transfers between devices, local(): x_other = lax.ppermute(x_give, 'pipe', swap)  5.64 us
    ppermute x1, starting transfers between devices, local(): kg_other = lax.ppermute(kg_give, 'pipe', swap)  4.82 us
  transfers between devices with their start and end apart: 8, of which 3 were waited for; matrix products, arithmetic and copies ran while one was open for 2% of the time, Pallas kernels for 5%

profile of v2, /device:TPU:1, one launch (start us, length us, event | category | flops | bytes accessed | tf_op | source)
XLA Modules:
  0.0 135.8 jit_solution(15899893771932016928)
XLA Ops:
  0.6 0.0 copy-start
  0.6 0.0 copy-start.1
  0.7 0.0 copy-start.2
  0.7 0.0 copy-start.3
  0.7 0.0 copy-start.4
  0.7 1.2 dynamic-slice_bitcast_fusion
  2.0 5.6 %collective-permute-start = (bf16[128,1536]{1,0:T(8,128)(2,1)S(1)}, bf16[128,1536]{1,0:T(8,128)(2,1)S(1)}, u32[]{:S(2)}, u32[]{:S(2)}) collective-permute-start(bf16[128,1536]{1,0:T(8,128)(2,1)S(1)} %get-tuple-element.18), channel_id=1, source_target_pairs={{0,64},{64,0},{128,192},{192,128},{256,320},{320,256},{384,448},{4... | collective-permute-start | bytes 1179656 | tf_op jit(solution)/shard_map/ppermute | solution.py:321
  7.6 0.0 copy-done.1
  7.6 0.0 copy-done.2
  7.7 0.0 copy-done.3
  7.7 1.9 %collective-permute-start.1 = (f32[33,1536]{1,0:T(8,128)S(1)}, f32[33,1536]{1,0:T(8,128)S(1)}, u32[]{:S(2)}, u32[]{:S(2)}) collective-permute-start(f32[33,1536]{1,0:T(8,128)S(1)} %pad_maximum_fusion.w_ref.refs_3_.refs_4_.refs_5_.refs_6_), channel_id=1, source_target_pairs={{0,64},{64,0},{128,192},{192,128},{256,320},{320,256},{384,448},{4... | collective-permute-start | bytes 608264 | tf_op jit(solution)/shard_map/ppermute | solution.py:320
  9.6 0.0 copy-done.4
  9.6 0.6 constant_dynamic-slice_fusion
  10.2 0.7 stack.31.len_ref.info_ref
  11.0 3.1 %forward.2.refs_1_.refs_2_.refs_3_.refs_4_ = f32[25,128,128]{2,1,0:T(8,128)S(1)} custom-call(s32[5]{0:T(128)S(1)} %stack.31.len_ref.info_ref, bf16[128,1536]{1,0:T(8,128)(2,1)S(1)} %get-tuple-element.19.x_ref, f32[33,1536]{1,0:T(8,128)S(1)} %pad_maximum_fusion.w_ref.refs_3_.refs_4_.refs_5_.refs_6_), custom_call_target="tpu_custom_call" | custom-call | flops 19660800 | bytes 3145728 | tf_op jit(solution)/shard_map/forward/pallas_call | solution.py:82
  14.0 0.0 copy-done
  14.1 4.4 %collective-permute-done.1.w_ref.refs_4_.refs_5_.refs_6_.refs_7_ = f32[33,1536]{1,0:T(8,128)S(1)} collective-permute-done((f32[33,1536]{1,0:T(8,128)S(1)}, f32[33,1536]{1,0:T(8,128)S(1)}, u32[]{:S(2)}, u32[]{:S(2)}) %collective-permute-start.1) | collective-permute-done | bytes 202784 | tf_op jit(solution)/shard_map/ppermute | solution.py:320
  18.5 0.0 collective-permute-done.x_ref
  18.5 3.1 %forward.3.refs_2_.refs_3_.refs_4_.refs_5_ = f32[25,128,128]{2,1,0:T(8,128)S(1)} custom-call(s32[5]{0:T(128)S(1)} %stack.31.len_ref.info_ref, bf16[128,1536]{1,0:T(8,128)(2,1)S(1)} %collective-permute-done.x_ref, f32[33,1536]{1,0:T(8,128)S(1)} %collective-permute-done.1.w_ref.refs_4_.refs_5_.refs_6_.refs_7_), custom_call_target="tpu_custom_call" | custom-call | flops 19660800 | bytes 3145728 | tf_op jit(solution)/shard_map/forward/pallas_call | solution.py:82
  21.5 6.7 %phase.3 = bf16[128,1536]{1,0:T(8,128)(2,1)S(1)} custom-call(s32[5]{0:T(128)S(1)} %stack.31.len_ref.info_ref, bf16[128,1536]{1,0:T(8,128)(2,1)S(1)} %dynamic-slice_bitcast_fusion.2.refs_0_, f32[25,128,128]{2,1,0:T(8,128)S(1)} %forward.2.refs_1_.refs_2_.refs_3_.refs_4_, f32[25,128,128]{2,1,0:T(8,128)S(1)} %forward.3.refs_2_.refs_3_.refs_4_.refs_5_, ...), custom_call_target="tpu_custom_call" | custom-call | flops 31457280 | bytes 5242880 | tf_op jit(solution)/shard_map/phase/pallas_call | solution.py:215
  28.2 0.7 collective-permute-start.2
  28.9 0.0 collective-permute-done.2.refs_1_
  29.0 6.7 %phase.4 = bf16[128,1536]{1,0:T(8,128)(2,1)S(1)} custom-call(s32[5]{0:T(128)S(1)} %stack.31.len_ref.info_ref, bf16[128,1536]{1,0:T(8,128)(2,1)S(1)} %dynamic-slice_bitcast_fusion.2.refs_0_, bf16[128,1536]{1,0:T(8,128)(2,1)S(1)} %collective-permute-done.2.refs_1_, f32[25,128,128]{2,1,0:T(8,128)S(1)} %forward.2.refs_1_.refs_2_.refs_3_.refs_4_, ...), custom_call_target="tpu_custom_call" | custom-call | flops 31457280 | bytes 5242880 | tf_op jit(solution)/shard_map/phase/pallas_call | solution.py:215
  35.7 0.7 collective-permute-start.3
  36.4 0.0 collective-permute-done.3.refs_2_
  36.4 6.7 %phase.5 = bf16[128,1536]{1,0:T(8,128)(2,1)S(1)} custom-call(s32[5]{0:T(128)S(1)} %stack.31.len_ref.info_ref, bf16[128,1536]{1,0:T(8,128)(2,1)S(1)} %dynamic-slice_bitcast_fusion.2.refs_0_, bf16[128,1536]{1,0:T(8,128)(2,1)S(1)} %collective-permute-done.2.refs_1_, bf16[128,1536]{1,0:T(8,128)(2,1)S(1)} %collective-permute-done.3.refs_2_, ...), custom_call_target="tpu_custom_call" | custom-call | flops 31457280 | bytes 5242880 | tf_op jit(solution)/shard_map/phase/pallas_call | solution.py:215
  43.1 1.3 collective-permute-start.4
  44.4 29.9 %collective-permute-done.4.refs_3_ = bf16[128,1536]{1,0:T(8,128)(2,1)S(1)} collective-permute-done((bf16[128,1536]{1,0:T(8,128)(2,1)S(1)}, bf16[128,1536]{1,0:T(8,128)(2,1)S(1)}, u32[]{:S(2)}, u32[]{:S(2)}) %collective-permute-start.4) | collective-permute-done | bytes 393248 | tf_op jit(solution)/shard_map/ppermute | solution.py:330
  74.3 7.1 %phase_last.1 = (bf16[128,1536]{1,0:T(8,128)(2,1)S(1)}, bf16[128,1536]{1,0:T(8,128)(2,1)S(1)}, f32[2,8,1536]{2,1,0:T(8,128)S(1)}, f32[2,12,128,128]{3,2,1,0:T(8,128)S(1)}) custom-call(s32[5]{0:T(128)S(1)} %stack.31.len_ref.info_ref, bf16[128,1536]{1,0:T(8,128)(2,1)S(1)} %dynamic-slice_bitcast_fusion.2.refs_0_, ...), custom_call_target="tpu_custom_call" | custom-call | flops 31457280 | bytes 5242880 | tf_op jit(solution)/shard_map/phase_last/pallas_call | solution.py:215
  81.4 4.2 %kernel_grad.3 = bf16[64,8,128]{2,1,0:T(8,128)(2,1)S(1)} custom-call(s32[5]{0:T(128)S(1)} %stack.31.len_ref.info_ref, bf16[128,1536]{1,0:T(8,128)(2,1)S(1)} %collective-permute-done.x_ref, f32[2,12,128,128]{3,2,1,0:T(8,128)S(1)} %get-tuple-element.13.dh_ref, f32[2,8,1536]{2,1,0:T(8,128)S(1)} %get-tuple-element.14.gb_ref), custom_call_target="tpu_custom_call" | custom-call | flops 12189696 | bytes 2097152 | tf_op jit(solution)/shard_map/kernel_grad/pallas_call | solution.py:261
  85.6 4.8 %collective-permute-start.6 = (bf16[64,8,128]{2,1,0:T(8,128)(2,1)S(1)}, bf16[64,8,128]{2,1,0:T(8,128)(2,1)S(1)}, u32[]{:S(2)}, u32[]{:S(2)}) collective-permute-start(bf16[64,8,128]{2,1,0:T(8,128)(2,1)S(1)} %kernel_grad.3), channel_id=1, source_target_pairs={{0,64},{64,0},{128,192},{192,128},{256,320},{320,256},{384,448},{4... | collective-permute-start | bytes 393224 | tf_op jit(solution)/shard_map/ppermute | solution.py:333
  90.4 2.0 %collective-permute-start.5 = (bf16[128,1536]{1,0:T(8,128)(2,1)S(1)}, bf16[128,1536]{1,0:T(8,128)(2,1)S(1)}, u32[]{:S(2)}, u32[]{:S(2)}) collective-permute-start(bf16[128,1536]{1,0:T(8,128)(2,1)S(1)} %get-tuple-element.12), channel_id=1, source_target_pairs={{0,64},{64,0},{128,192},{192,128},{256,320},{320,256},{384,448},{4... | collective-permute-start | bytes 1179656 | tf_op jit(solution)/shard_map/ppermute | solution.py:337
  92.4 4.2 %kernel_grad.2 = f32[64,8,128]{2,1,0:T(8,128)S(1)} custom-call(s32[5]{0:T(128)S(1)} %stack.31.len_ref.info_ref, bf16[128,1536]{1,0:T(8,128)(2,1)S(1)} %get-tuple-element.19.x_ref, f32[2,12,128,128]{3,2,1,0:T(8,128)S(1)} %get-tuple-element.13.dh_ref, f32[2,8,1536]{2,1,0:T(8,128)S(1)} %get-tuple-element.14.gb_ref), custom_call_target="tpu_custom_call" | custom-call | flops 12189696 | bytes 2097152 | tf_op jit(solution)/shard_map/kernel_grad/pallas_call | solution.py:261
  96.6 0.0 collective-permute-done.6
  96.6 0.7 add_convert_fusion
  97.3 20.8 %all-to-all-start = ((bf16[64,8,128]{2,1,0:T(8,128)(2,1)}), bf16[64,8,128]{2,1,0:T(8,128)(2,1)S(1)}, u32[]{:S(2)}, u32[]{:S(2)}) async-start(bf16[64,8,128]{2,1,0:T(8,128)(2,1)} %add_convert_fusion), calls=%async_computation | async-start | bytes 262144 | tf_op jit(solution)/shard_map/all_to_all | solution.py:336
  118.0 0.0 collective-permute-done.5
  118.1 1.0 maximum_select_fusion
  119.1 16.1 %all-to-all-done.parts_ref = bf16[64,8,128]{2,1,0:T(8,128)(2,1)S(1)} async-done(((bf16[64,8,128]{2,1,0:T(8,128)(2,1)}), bf16[64,8,128]{2,1,0:T(8,128)(2,1)S(1)}, u32[]{:S(2)}, u32[]{:S(2)}) %all-to-all-start) | async-done | bytes 131104 | tf_op jit(solution)/shard_map/all_to_all | solution.py:336
  135.1 0.7 finish.1
  (3 shorter events, 0.1 us)
Async XLA Ops:
  0.6 13.4 %copy-start = (bf16[2,1,128,1536]{3,2,1,0:T(8,128)(2,1)S(1)}, bf16[2,1,128,1536]{3,2,1,0:T(8,128)(2,1)}, u32[]{:S(2)}) copy-start(bf16[2,1,128,1536]{3,2,1,0:T(8,128)(2,1)} %param.7) | copy-start | bytes 2359300
  0.6 7.0 %copy-start.1 = (bf16[1,31,1536]{2,1,0:T(8,128)(2,1)S(1)}, bf16[1,31,1536]{2,1,0:T(8,128)(2,1)}, u32[]{:S(2)}) copy-start(bf16[1,31,1536]{2,1,0:T(8,128)(2,1)} %param.9) | copy-start | bytes 285700
  0.7 7.0 %copy-start.2 = (f32[1,1536]{1,0:T(1,128)S(1)}, f32[1,1536]{1,0:T(1,128)}, u32[]{:S(2)}) copy-start(f32[1,1536]{1,0:T(1,128)} %param.11) | copy-start | bytes 18436
  0.7 7.0 %copy-start.3 = (f32[1,1536]{1,0:T(1,128)S(1)}, f32[1,1536]{1,0:T(1,128)}, u32[]{:S(2)}) copy-start(f32[1,1536]{1,0:T(1,128)} %param.10) | copy-start | bytes 18436
  0.7 9.0 %copy-start.4 = (s32[2,1]{0,1:T(1,128)S(1)}, s32[2,1]{0,1:T(1,128)}, u32[]{:S(2)}) copy-start(s32[2,1]{0,1:T(1,128)} %param.8) | copy-start | bytes 28
  2.0 16.5 %collective-permute-start = (bf16[128,1536]{1,0:T(8,128)(2,1)S(1)}, bf16[128,1536]{1,0:T(8,128)(2,1)S(1)}, u32[]{:S(2)}, u32[]{:S(2)}) collective-permute-start(bf16[128,1536]{1,0:T(8,128)(2,1)S(1)} %get-tuple-element.18), channel_id=1, source_target_pairs={{0,64},{64,0},{128,192},{192,128},{256,320},{320,256},{384,448},{4... | collective-permute-start | bytes 1179656 | tf_op jit(solution)/shard_map/ppermute | solution.py:321
  7.7 10.8 %collective-permute-start.1 = (f32[33,1536]{1,0:T(8,128)S(1)}, f32[33,1536]{1,0:T(8,128)S(1)}, u32[]{:S(2)}, u32[]{:S(2)}) collective-permute-start(f32[33,1536]{1,0:T(8,128)S(1)} %pad_maximum_fusion.w_ref.refs_3_.refs_4_.refs_5_.refs_6_), channel_id=1, source_target_pairs={{0,64},{64,0},{128,192},{192,128},{256,320},{320,256},{384,448},{4... | collective-permute-start | bytes 608264 | tf_op jit(solution)/shard_map/ppermute | solution.py:320
  28.2 0.7 collective-permute-start.2
  35.7 0.7 collective-permute-start.3
  43.1 31.2 %collective-permute-start.4 = (bf16[128,1536]{1,0:T(8,128)(2,1)S(1)}, bf16[128,1536]{1,0:T(8,128)(2,1)S(1)}, u32[]{:S(2)}, u32[]{:S(2)}) collective-permute-start(bf16[128,1536]{1,0:T(8,128)(2,1)S(1)} %phase.5), channel_id=1, source_target_pairs={{192,64},{128,0},{193,65},{129,1},{194,66},{130,2},{195,67},{131,3... | collective-permute-start | bytes 1179656 | tf_op jit(solution)/shard_map/ppermute | solution.py:330
  85.6 11.0 %collective-permute-start.6 = (bf16[64,8,128]{2,1,0:T(8,128)(2,1)S(1)}, bf16[64,8,128]{2,1,0:T(8,128)(2,1)S(1)}, u32[]{:S(2)}, u32[]{:S(2)}) collective-permute-start(bf16[64,8,128]{2,1,0:T(8,128)(2,1)S(1)} %kernel_grad.3), channel_id=1, source_target_pairs={{0,64},{64,0},{128,192},{192,128},{256,320},{320,256},{384,448},{4... | collective-permute-start | bytes 393224 | tf_op jit(solution)/shard_map/ppermute | solution.py:333
  90.4 27.6 %collective-permute-start.5 = (bf16[128,1536]{1,0:T(8,128)(2,1)S(1)}, bf16[128,1536]{1,0:T(8,128)(2,1)S(1)}, u32[]{:S(2)}, u32[]{:S(2)}) collective-permute-start(bf16[128,1536]{1,0:T(8,128)(2,1)S(1)} %get-tuple-element.12), channel_id=1, source_target_pairs={{0,64},{64,0},{128,192},{192,128},{256,320},{320,256},{384,448},{4... | collective-permute-start | bytes 1179656 | tf_op jit(solution)/shard_map/ppermute | solution.py:337
  97.3 37.8 %all-to-all-start = ((bf16[64,8,128]{2,1,0:T(8,128)(2,1)}), bf16[64,8,128]{2,1,0:T(8,128)(2,1)S(1)}, u32[]{:S(2)}, u32[]{:S(2)}) async-start(bf16[64,8,128]{2,1,0:T(8,128)(2,1)} %add_convert_fusion), calls=%async_computation | async-start | bytes 262144 | tf_op jit(solution)/shard_map/all_to_all | solution.py:336

commit v3 on v2

--- a/solution.py
+++ b/solution.py
@@ -14,6 +14,7 @@
 PADDED = 160
 EPS = 1e-05
 ROWS = 40
+TABLE = 48
 F32 = jnp.float32
 BF16 = jnp.bfloat16
 VMEM = pl.BlockSpec(memory_space=pltpu.VMEM)
@@ -39,10 +40,90 @@
     pad_ref[:, LEAD + frames :, :] = jnp.zeros((pad_ref.shape[0], tail, LANES), F32)
 
 
-def forward_kernel(len_ref, x_ref, w_ref, s_ref, pad_ref):
+def upper_of(place_ref):
+    return lax.rem(place_ref[0], 2)
+
+
+def thirds(value):
+    high = value.astype(BF16).astype(F32)
+    middle = (value - high).astype(BF16).astype(F32)
+    return [high, middle, value - high - middle]
+
+
+def message_kernel(place_ref, x_ref, kernel_ref, gain_ref, bias_ref, message_ref, w_ref):
+    frames, width = x_ref.shape[1:]
+    filler = jnp.zeros((TABLE - KW - 6, LANES), F32)
+
+    def copy(b, carry):
+        cols = columns(b)
+        message_ref[:frames, cols] = x_ref[0, :, cols]
+        kernel = kernel_ref[:, cols].astype(F32)
+        gain, bias = gain_ref[:, cols], bias_ref[:, cols]
+        table = jnp.concatenate([kernel] + thirds(gain) + thirds(bias) + [filler], 0)
+        message_ref[frames:, cols] = table.astype(BF16)
+        w_ref[:, cols] = jnp.concatenate([kernel, gain, bias], 0)
+        return carry
+
+    lax.fori_loop(0, width // LANES, copy, 0)
+
+
+def whole(*shape):
+    return pl.BlockSpec(shape, lambda i, *s: (0,) * len(shape))
+
+
+def message(place, saved, kernel, gain, bias, limit=8 << 20):
+    frames, width = saved.shape[1:]
+    return pl.pallas_call(
+        message_kernel,
+        grid_spec=pltpu.PrefetchScalarGridSpec(
+            num_scalar_prefetch=1,
+            grid=(1,),
+            in_specs=[
+                pl.BlockSpec((1, frames, width), lambda i, p: (lax.rem(p[0], 2), 0, 0)),
+                whole(KW, width),
+                whole(1, width),
+                whole(1, width),
+            ],
+            out_specs=[whole(frames + TABLE, width), whole(KW + 2, width)],
+        ),
+        out_shape=[
+            jax.ShapeDtypeStruct((frames + TABLE, width), BF16),
+            jax.ShapeDtypeStruct((KW + 2, width), F32),
+        ],
+        compiler_params=pltpu.CompilerParams(vmem_limit_bytes=limit),
+        cost_estimate=pl.CostEstimate(flops=width * 400, bytes_accessed=1 << 20, transcendentals=0),
+        name="message",
+    )(place, saved, kernel, gain, bias)
+
+
+def decode(table_ref, w_ref):
+    frames = table_ref.shape[0] - TABLE
+
+    def expand(b, carry):
+        cols = columns(b)
+        table = table_ref[frames:, cols].astype(F32)
+        gain = table[KW : KW + 1] + table[KW + 1 : KW + 2] + table[KW + 2 : KW + 3]
+        bias = table[KW + 3 : KW + 4] + table[KW + 4 : KW + 5] + table[KW + 5 : KW + 6]
+        w_ref[:, cols] = jnp.concatenate([table[:KW], gain, bias], 0)
+        return carry
+
+    lax.fori_loop(0, table_ref.shape[1] // LANES, expand, 0)
+
+
+def forward_local_kernel(place_ref, lens_ref, x_ref, w_ref, s_ref, pad_ref):
+    forward_body(lens_ref[1 - upper_of(place_ref)], x_ref.at[0], w_ref, s_ref, pad_ref)
+
+
+def forward_other_kernel(place_ref, lens_ref, message_ref, s_ref, w_ref, pad_ref):
+    frames = message_ref.shape[0] - TABLE
+    decode(message_ref, w_ref)
+    forward_body(lens_ref[1 - upper_of(place_ref)], message_ref.at[pl.ds(0, frames)], w_ref, s_ref, pad_ref)
+
+
+def forward_body(length, x_ref, w_ref, s_ref, pad_ref):
     frames, width = x_ref.shape
     blocks = width // LANES
-    mask = live(len_ref[0], frames)
+    mask = live(length, frames)
     clear_margins(pad_ref, frames)
     zero = jnp.zeros((frames, LANES), F32)
 
@@ -76,19 +157,37 @@
     lax.fori_loop(0, blocks, activate, 0)
 
 
-def forward(length, x, w, limit=16 << 20):
-    frames, width = x.shape
+def forward(place, lens, x, w, limit=16 << 20):
+    frames, width = (x.shape[0] - TABLE, x.shape[1]) if w is None else x.shape[1:]
     blocks = width // LANES
-    return pl.pallas_call(
-        forward_kernel,
-        out_shape=jax.ShapeDtypeStruct((2 * blocks + 1, frames, LANES), F32),
-        in_specs=[SMEM, VMEM, VMEM],
-        out_specs=VMEM,
-        scratch_shapes=[pltpu.VMEM((blocks, PADDED, LANES), F32)],
+    stats = (2 * blocks + 1, frames, LANES)
+    if w is None:
+        body, operands = forward_other_kernel, (x,)
+        in_specs = [whole(frames + TABLE, width)]
+        out_specs = [whole(*stats), whole(KW + 2, width)]
+        out_shape = [jax.ShapeDtypeStruct(stats, F32), jax.ShapeDtypeStruct((KW + 2, width), F32)]
+    else:
+        body, operands = forward_local_kernel, (x, w)
+        in_specs = [
+            pl.BlockSpec((1, frames, width), lambda i, p, n: (1 - lax.rem(p[0], 2), 0, 0)),
+            whole(KW + 2, width),
+        ]
+        out_specs = whole(*stats)
+        out_shape = jax.ShapeDtypeStruct(stats, F32)
+    return pl.pallas_call(
+        body,
+        grid_spec=pltpu.PrefetchScalarGridSpec(
+            num_scalar_prefetch=2,
+            grid=(1,),
+            in_specs=in_specs,
+            out_specs=out_specs,
+            scratch_shapes=[pltpu.VMEM((blocks, PADDED, LANES), F32)],
+        ),
+        out_shape=out_shape,
         compiler_params=pltpu.CompilerParams(vmem_limit_bytes=limit),
         cost_estimate=pl.CostEstimate(flops=frames * width * 100, bytes_accessed=3 << 20, transcendentals=frames * width),
-        name="forward",
-    )(length, x, w)
+        name="forward_other" if w is None else "forward_local",
+    )(place, lens, *operands)
 
 
 def section(i, mask, dy_ref, s_ref, w_ref, pad_ref, dx_ref, gb_ref, dh_ref):
@@ -127,7 +226,7 @@
     lax.fori_loop(0, blocks, convolve, 0)
 
 
-def phase_kernel(n_dy, last, info_ref, *refs):
+def phase_kernel(n_dy, last, stages, place_ref, lens_ref, *refs):
     dys = refs[:n_dy]
     s_local, s_other, w_local, w_other = refs[n_dy : n_dy + 4]
     refs = refs[n_dy + 4 :]
@@ -138,7 +237,10 @@
         dx_ref = refs[0]
         dy_ref, first_ref, s_ref, w_ref, pad_ref, sem = refs[1:]
         gb_ref = dh_ref = None
-    length, stage, local_first = info_ref[0], info_ref[1], info_ref[2]
+    local_first = upper_of(place_ref)
+    item = 1 - local_first
+    length = lens_ref[item]
+    stage = stages - 1 - lax.div(place_ref[0], 2)
     frames = dy_ref.shape[0]
 
     def fetch(a, b):
@@ -154,7 +256,7 @@
 
         @pl.when(chosen == k)
         def _():
-            pltpu.make_async_copy(dys[k], dy_ref, sem.at[0]).start()
+            pltpu.make_async_copy(dys[k] if k else dys[k].at[item], dy_ref, sem.at[0]).start()
 
     ahead = fetch((w_local, s_local), (w_other, s_other))
     behind = fetch((w_other, s_other), (w_local, s_local))
@@ -171,7 +273,7 @@
 
     clear_margins(pad_ref, frames)
     mask = live(length, frames)
-    pltpu.make_async_copy(dys[0], dy_ref, sem.at[0]).wait()
+    pltpu.make_async_copy(dys[0].at[item], dy_ref, sem.at[0]).wait()
     ahead[0].wait()
     ahead[1].wait()
     section(0, mask, dy_ref, s_ref, w_ref, pad_ref, first_ref, gb_ref, dh_ref)
@@ -191,8 +293,8 @@
             give_ref[...] = first_ref[...]
 
 
-def phase(info, dys, s_local, s_other, w_local, w_other, last, limit=20 << 20):
-    frames, width = dys[0].shape
+def phase(place, lens, stages, dys, s_local, s_other, w_local, w_other, last, limit=20 << 20):
+    frames, width = dys[0].shape[1:]
     blocks = width // LANES
     dx = jax.ShapeDtypeStruct((frames, width), BF16)
     out_shape = [dx]
@@ -213,29 +315,28 @@
         ]
         scratch.append(pltpu.VMEM((frames, width), BF16))
     return pl.pallas_call(
-        functools.partial(phase_kernel, len(dys), last),
+        functools.partial(phase_kernel, len(dys), last, stages),
         out_shape=out_shape,
-        in_specs=[SMEM] + [ANY] * (len(dys) + 4),
+        in_specs=[SMEM, SMEM] + [ANY] * (len(dys) + 4),
         out_specs=[VMEM] * len(out_shape),
         scratch_shapes=scratch,
         compiler_params=pltpu.CompilerParams(vmem_limit_bytes=limit),
         cost_estimate=pl.CostEstimate(flops=frames * width * 160, bytes_accessed=5 << 20, transcendentals=0),
         name="phase_last" if last else "phase",
-    )(info, *dys, s_local, s_other, w_local, w_other)
-
-
-def kernel_grad_kernel(rows, info_ref, x_ref, dh_ref, gb_ref, out_ref, pad_ref, turned_ref):
-    frames, width = x_ref.shape
-    blocks = width // LANES
-    members = out_ref.shape[0]
-    share = width // members
-    mask = live(info_ref[0], frames)
+    )(place, lens, *dys, s_local, s_other, w_local, w_other)
+
+
+def kernel_grad_kernel(place_ref, lens_ref, x_ref, dh_ref, gb_ref, out_ref, pad_ref):
+    frames = dh_ref.shape[2]
+    blocks = dh_ref.shape[1]
+    mask = live(lens_ref[1 - upper_of(place_ref)], frames)
     clear_margins(pad_ref, frames)
-    filler = jnp.zeros((LANES - KW - 2, LANES), F32)
+    filler = jnp.zeros((ROWS - KW - 2, LANES), F32)
 
     def correlate(b, carry):
         cols = columns(b)
-        pad_ref[b, LEAD : LEAD + frames, :] = jnp.where(mask, x_ref[:, cols].astype(F32), 0.0)
+        x = x_ref[:frames, cols] if len(x_ref.shape) == 2 else x_ref[0, :, cols]
+        pad_ref[b, LEAD : LEAD + frames, :] = jnp.where(mask, x.astype(F32), 0.0)
         dh = dh_ref[0, b]
         sums = []
         for j in range(KW):
@@ -243,10 +344,50 @@
             sums.append(jnp.sum(product, 0, keepdims=True))
         sums.append(gb_ref[0, 0:1, cols])
         sums.append(gb_ref[0, 1:2, cols])
-        turned_ref[cols, :] = jnp.concatenate(sums + [filler], 0).T
+        out_ref[:, cols] = jnp.concatenate(sums + [filler], 0).astype(out_ref.dtype)
         return carry
 
     lax.fori_loop(0, blocks, correlate, 0)
+
+
+def kernel_grad(place, lens, x, dh, gb, own, limit=16 << 20):
+    blocks, frames = dh.shape[1:3]
+    width = blocks * LANES
+    if own:
+        x_spec = pl.BlockSpec((1, frames, width), lambda i, p, n: (1 - lax.rem(p[0], 2), 0, 0))
+        which = lambda p: 1 - lax.rem(p[0], 2)
+    else:
+        x_spec = whole(*x.shape)
+        which = lambda p: lax.rem(p[0], 2)
+    return pl.pallas_call(
+        kernel_grad_kernel,
+        grid_spec=pltpu.PrefetchScalarGridSpec(
+            num_scalar_prefetch=2,
+            grid=(1,),
+            in_specs=[
+                x_spec,
+                pl.BlockSpec((1, blocks, frames, LANES), lambda i, p, n: (which(p), 0, 0, 0)),
+                pl.BlockSpec((1, 8, width), lambda i, p, n: (which(p), 0, 0)),
+            ],
+            out_specs=whole(ROWS, width),
+            scratch_shapes=[pltpu.VMEM((blocks, PADDED, LANES), F32)],
+        ),
+        out_shape=jax.ShapeDtypeStruct((ROWS, width), F32 if own else BF16),
+        compiler_params=pltpu.CompilerParams(vmem_limit_bytes=limit),
+        cost_estimate=pl.CostEstimate(flops=frames * width * 62, bytes_accessed=2 << 20, transcendentals=0),
+        name="kernel_grad_own" if own else "kernel_grad_other",
+    )(place, lens, x, dh, gb)
+
+
+def pack_kernel(own_ref, other_ref, out_ref, turned_ref):
+    rows, width = own_ref.shape
+    members = out_ref.shape[0]
+    share = width // members
+    filler = jnp.zeros((LANES - rows, LANES), F32)
+    for b in range(width // LANES):
+        cols = pl.ds(b * LANES, LANES)
+        total = own_ref[:, cols] + other_ref[:, cols].astype(F32)
+        turned_ref[cols, :] = jnp.concatenate([total, filler], 0).T
     for d in range(members):
         start = d * share
         packed = turned_ref[start : start + 8, :]
@@ -255,27 +396,18 @@
         out_ref[d] = packed.astype(out_ref.dtype)
 
 
-def kernel_grad(info, x, dh, gb, which, members, dtype, limit=16 << 20):
-    frames, width = x.shape
-    blocks = width // LANES
-    return pl.pallas_call(
-        functools.partial(kernel_grad_kernel, ROWS),
-        grid_spec=pltpu.PrefetchScalarGridSpec(
-            num_scalar_prefetch=1,
-            grid=(1,),
-            in_specs=[
-                pl.BlockSpec((frames, width), lambda i, s: (0, 0)),
-                pl.BlockSpec((1, blocks, frames, LANES), lambda i, s: (s[which], 0, 0, 0)),
-                pl.BlockSpec((1, 8, width), lambda i, s: (s[which], 0, 0)),
-            ],
-            out_specs=pl.BlockSpec((members, 8, LANES), lambda i, s: (0, 0, 0)),
-            scratch_shapes=[pltpu.VMEM((blocks, PADDED, LANES), F32), pltpu.VMEM((width, LANES), F32)],
-        ),
-        out_shape=jax.ShapeDtypeStruct((members, 8, LANES), dtype),
-        compiler_params=pltpu.CompilerParams(vmem_limit_bytes=limit),
-        cost_estimate=pl.CostEstimate(flops=frames * width * 62, bytes_accessed=2 << 20, transcendentals=0),
-        name="kernel_grad",
-    )(info, x, dh, gb)
+def pack(own, other, members, limit=8 << 20):
+    width = own.shape[1]
+    return pl.pallas_call(
+        pack_kernel,
+        out_shape=jax.ShapeDtypeStruct((members, 8, LANES), BF16),
+        in_specs=[VMEM, VMEM],
+        out_specs=VMEM,
+        scratch_shapes=[pltpu.VMEM((width, LANES), F32)],
+        compiler_params=pltpu.CompilerParams(vmem_limit_bytes=limit),
+        cost_estimate=pl.CostEstimate(flops=width * 256, bytes_accessed=1 << 19, transcendentals=0),
+        name="pack",
+    )(own, other)
 
 
 def finish_kernel(rows, parts_ref, kernel_ref, gain_ref, bias_ref):
@@ -307,32 +439,27 @@
 def local(saved, out_grad, lengths, kernel, gain, bias):
     sections = lax.axis_size("pipe")
     members = lax.axis_size("dp")
-    place = lax.axis_index("pipe")
-    upper = place % 2
-    item = 1 - upper
+    place = lax.axis_index("pipe").astype(jnp.int32)
+    item = 1 - place % 2
+    place = jnp.reshape(place, (1,))
+    lens = lengths[:, 0]
     stages = sections // 2
-    stage = stages - 1 - place // 2
     swap = [(p, p ^ 1) for p in range(sections)]
-    x_both = saved[0, :, 0]
-    x_give = lax.dynamic_index_in_dim(x_both, 1 - item, 0, keepdims=False)
-    x_local = lax.dynamic_index_in_dim(x_both, item, 0, keepdims=False)
-    w_local = jnp.concatenate([kernel[0].astype(F32), gain, bias], 0)
-    w_other = lax.ppermute(w_local, "pipe", swap)
-    x_other = lax.ppermute(x_give, "pipe", swap)
-    dys = [lax.dynamic_index_in_dim(out_grad[:, 0], item, 0, keepdims=False)]
-    length = lax.dynamic_index_in_dim(lengths[:, 0], item, 0, keepdims=False)
-    info = jnp.stack([length, stage, upper, 1 - upper, upper]).astype(jnp.int32)
-    s_local = forward(info, x_local, w_local)
-    s_other = forward(info, x_other, w_other)
+    saved = saved[0, :, 0]
+    sent, w_local = message(place, saved, kernel[0], gain, bias)
+    came = lax.ppermute(sent, "pipe", swap)
+    dys = [out_grad[:, 0]]
+    s_local = forward(place, lens, saved, w_local)
+    s_other, w_other = forward(place, lens, came, None)
     for k in range(stages - 1):
-        (dx,) = phase(info, dys, s_local, s_other, w_local, w_other, False)
+        (dx,) = phase(place, lens, stages, dys, s_local, s_other, w_local, w_other, False)
         top = sections - 1 - 2 * k
         dys.append(lax.ppermute(dx, "pipe", [(top, top - 2), (top - 1, top - 3)]))
-    own, give, gb, dh = phase(info, dys, s_local, s_other, w_local, w_other, True)
-    kg_give = kernel_grad(info, x_other, dh, gb, 4, members, BF16)
+    own, give, gb, dh = phase(place, lens, stages, dys, s_local, s_other, w_local, w_other, True)
+    kg_give = kernel_grad(place, lens, came, dh, gb, False)
     kg_other = lax.ppermute(kg_give, "pipe", swap)
-    kg_own = kernel_grad(info, x_local, dh, gb, 3, members, F32)
-    packed = (kg_own + kg_other.astype(F32)).astype(BF16)
+    kg_own = kernel_grad(place, lens, saved, dh, gb, True)
+    packed = pack(kg_own, kg_other, members)
     parts = lax.all_to_all(packed, "dp", 0, 0, tiled=True)
     dx_other = lax.ppermute(give, "pipe", swap)
     kernel_part, gain_part, bias_part = finish(parts, kernel.shape[2] // members)

time: 136 us -> 137 us (level)
  local copies, waits for them, and re-layouts: 2.62 us -> 5.2 us
  starting transfers between devices: 37.8 us -> 35.3 us
  waiting for transfers between devices: 50.4 us -> 52.9 us
    unnamed x10 -> x18, local copies, waits for them, and re-layouts: 0.03 us -> 5.2 us
    ppermute x1, waiting for transfers between devices: 0.01 us -> 3.05 us  [local(): kg_other = lax.ppermute(kg_give, 'pipe', swap)]
    ppermute x1, starting transfers between devices: 1.96 us -> 4.95 us  [local(): dx_other = lax.ppermute(give, 'pipe', swap)]
    ppermute x1, starting transfers between devices: 4.82 us -> 1.96 us  [local(): kg_other = lax.ppermute(kg_give, 'pipe', swap)]
    ppermute x2 -> x1, starting transfers between devices: 7.56 us -> 5.77 us  [local(): came = lax.ppermute(sent, 'pipe', swap)]
    pallas_call x8 -> x10, Pallas kernels: 41.7 us -> 40.4 us  [the longest x4 27.2 us: phase(): pl.pallas_call(functools.partial(phase_kernel, len(dys), last, stages), o...]
    ppermute x2 -> x1, waiting for transfers between devices: 4.41 us -> 3.91 us  [local(): came = lax.ppermute(sent, 'pipe', swap)]
  transfers between devices with their start and end apart: 8 -> 7, of which waited for: 3 -> 4; matrix products, arithmetic and copies ran while one was open for 2% -> 1% of each run, Pallas kernels for 5% -> 7%
where the time goes in v3:
time: 137 us; the launch traced here: 136 us
  waiting for transfers between devices  52.9 us (39%)
  Pallas kernels  41.1 us (30%)
  starting transfers between devices  35.3 us (26%)
  local copies, waits for them, and re-layouts  5.2 us (4%)
    ppermute x3, waiting for transfers between devices, local(): dys.append(lax.ppermute(dx, 'pipe', [(top, top - 2), (top - 1, top - 3)]))  29.9 us
    pallas_call x4, Pallas kernels, phase(): pl.pallas_call(functools.partial(phase_kernel, len(dys), last, stages), o...  27.2 us
    all_to_all x1, starting transfers between devices, local(): parts = lax.all_to_all(packed, 'dp', 0, 0, tiled=True)  20 us
    all_to_all x1, waiting for transfers between devices, local(): parts = lax.all_to_all(packed, 'dp', 0, 0, tiled=True)  16 us
    pallas_call x2, Pallas kernels, forward(): pl.pallas_call(body, grid_spec=pltpu.PrefetchScalarGridSpec(num_scalar_pr...  6.23 us
    ppermute x1, starting transfers between devices, local(): came = lax.ppermute(sent, 'pipe', swap)  5.77 us
    pallas_call x2, Pallas kernels, kernel_grad(): pl.pallas_call(kernel_grad_kernel, grid_spec=pltpu.PrefetchScalarGridSpec...  5.68 us
    unnamed x18, local copies, waits for them, and re-layouts  5.2 us
  transfers between devices with their start and end apart: 7, of which 4 were waited for; matrix products, arithmetic and copies ran while one was open for 1% of the time, Pallas kernels for 7%

profile of v3, /device:TPU:1, one launch (start us, length us, event | category | flops | bytes accessed | tf_op | source)
XLA Modules:
  0.0 136.5 jit_solution(11927492333668562853)
XLA Ops:
  0.6 0.0 copy-start.1
  0.6 1.1 copy-done.1
  1.8 0.0 copy-start.4
  1.8 0.9 copy-done.4
  2.7 0.0 copy-start.7
  2.7 0.7 copy-done.7
  3.4 0.0 copy-start.8
  3.4 0.7 copy-done.8
  4.0 0.0 copy-start.6
  4.1 0.2 message.1
  4.3 0.0 copy-start
  4.3 5.8 %collective-permute-start = (bf16[176,1536]{1,0:T(8,128)(2,1)S(1)}, bf16[176,1536]{1,0:T(8,128)(2,1)S(1)}, u32[]{:S(2)}, u32[]{:S(2)}) collective-permute-start(bf16[176,1536]{1,0:T(8,128)(2,1)S(1)} %get-tuple-element.16), channel_id=1, source_target_pairs={{0,64},{64,0},{128,192},{192,128},{256,320},{320,256},{384,448},{4... | collective-permute-start | bytes 1622024 | tf_op jit(solution)/shard_map/ppermute | solution.py:450
  10.1 0.0 copy-start.2
  10.1 1.1 copy-done.2
  11.2 0.0 copy-start.5
  11.2 0.7 copy-done.5
  11.9 3.1 %forward_local.1.refs_1_.refs_2_.refs_3_.refs_4_ = f32[25,128,128]{2,1,0:T(8,128)S(1)} custom-call(s32[1]{0:T(128)} %bitcast.place_ref, s32[2]{0:T(128)S(1)} %bitcast.19, bf16[2,128,1536]{2,1,0:T(8,128)(2,1)S(1)} %bitcast.15, f32[33,1536]{1,0:T(8,128)S(1)} %get-tuple-element.15.w_ref.refs_3_.refs_4_.refs_5_.refs_6_), custom_call_target="tpu_custom_call" | custom-call | flops 19660800 | bytes 3145728 | tf_op jit(solution)/shard_map/forward_local/pallas_call | solution.py:177
  14.9 3.9 %collective-permute-done.message_ref.x_ref = bf16[176,1536]{1,0:T(8,128)(2,1)S(1)} collective-permute-done((bf16[176,1536]{1,0:T(8,128)(2,1)S(1)}, bf16[176,1536]{1,0:T(8,128)(2,1)S(1)}, u32[]{:S(2)}, u32[]{:S(2)}) %collective-permute-start) | collective-permute-done | bytes 540704 | tf_op jit(solution)/shard_map/ppermute | solution.py:450
  18.8 3.2 %forward_other.1 = (f32[25,128,128]{2,1,0:T(8,128)S(1)}, f32[33,1536]{1,0:T(8,128)S(1)}) custom-call(s32[1]{0:T(128)} %bitcast.place_ref, s32[2]{0:T(128)S(1)} %bitcast.20, bf16[176,1536]{1,0:T(8,128)(2,1)S(1)} %collective-permute-done.message_ref.x_ref), custom_call_target="tpu_custom_call" | custom-call | flops 19660800 | bytes 3145728 | tf_op jit(solution)/shard_map/forward_other/pallas_call | solution.py:177
  22.0 0.0 copy-done.6
  22.0 0.0 copy-done
  22.1 6.7 %phase.3 = bf16[128,1536]{1,0:T(8,128)(2,1)S(1)} custom-call(s32[1]{0:T(128)} %bitcast.place_ref, s32[2]{0:T(128)S(1)} %bitcast.21, bf16[2,128,1536]{2,1,0:T(8,128)(2,1)S(1)} %bitcast.10, f32[25,128,128]{2,1,0:T(8,128)S(1)} %forward_local.1.refs_1_.refs_2_.refs_3_.refs_4_, f32[25,128,128]{2,1,0:T(8,128)S(1)} %get-tuple-element.17.refs_2_.refs_3_.refs_4_.refs_5_, ...), custom_call_target="tpu_custom_call" | custom-call | flops 31457280 | bytes 5242880 | tf_op jit(solution)/shard_map/phase/pallas_call | solution.py:317
  28.8 0.7 collective-permute-start.1
  29.4 0.0 collective-permute-done.1.refs_1_
  29.5 6.7 %phase.4 = bf16[128,1536]{1,0:T(8,128)(2,1)S(1)} custom-call(s32[1]{0:T(128)} %bitcast.place_ref, s32[2]{0:T(128)S(1)} %bitcast.22, bf16[2,128,1536]{2,1,0:T(8,128)(2,1)S(1)} %bitcast.11, bf16[128,1536]{1,0:T(8,128)(2,1)S(1)} %collective-permute-done.1.refs_1_, f32[25,128,128]{2,1,0:T(8,128)S(1)} %forward_local.1.refs_1_.refs_2_.refs_3_.refs_4_, ...), custom_call_target="tpu_custom_call" | custom-call | flops 31457280 | bytes 5242880 | tf_op jit(solution)/shard_map/phase/pallas_call | solution.py:317
  36.2 0.7 collective-permute-start.2
  36.9 0.0 collective-permute-done.2.refs_2_
  36.9 6.7 %phase.5 = bf16[128,1536]{1,0:T(8,128)(2,1)S(1)} custom-call(s32[1]{0:T(128)} %bitcast.place_ref, s32[2]{0:T(128)S(1)} %bitcast.23, bf16[2,128,1536]{2,1,0:T(8,128)(2,1)S(1)} %bitcast.12, bf16[128,1536]{1,0:T(8,128)(2,1)S(1)} %collective-permute-done.1.refs_1_, bf16[128,1536]{1,0:T(8,128)(2,1)S(1)} %collective-permute-done.2.refs_2_, ...), custom_call_target="tpu_custom_call" | custom-call | flops 31457280 | bytes 5242880 | tf_op jit(solution)/shard_map/phase/pallas_call | solution.py:317
  43.6 1.3 collective-permute-start.3
  44.9 29.9 %collective-permute-done.3.refs_3_ = bf16[128,1536]{1,0:T(8,128)(2,1)S(1)} collective-permute-done((bf16[128,1536]{1,0:T(8,128)(2,1)S(1)}, bf16[128,1536]{1,0:T(8,128)(2,1)S(1)}, u32[]{:S(2)}, u32[]{:S(2)}) %collective-permute-start.3) | collective-permute-done | bytes 393248 | tf_op jit(solution)/shard_map/ppermute | solution.py:457
  74.8 7.1 %phase_last.1 = (bf16[128,1536]{1,0:T(8,128)(2,1)S(1)}, bf16[128,1536]{1,0:T(8,128)(2,1)S(1)}, f32[2,8,1536]{2,1,0:T(8,128)S(1)}, f32[2,12,128,128]{3,2,1,0:T(8,128)S(1)}) custom-call(s32[1]{0:T(128)} %bitcast.place_ref, s32[2]{0:T(128)S(1)} %bitcast.24, bf16[2,128,1536]{2,1,0:T(8,128)(2,1)S(1)} %bitcast.13, ...), custom_call_target="tpu_custom_call" | custom-call | flops 31457280 | bytes 5242880 | tf_op jit(solution)/shard_map/phase_last/pallas_call | solution.py:317
  81.9 0.0 copy-start.3
  81.9 5.0 %collective-permute-start.4 = (bf16[128,1536]{1,0:T(8,128)(2,1)S(1)}, bf16[128,1536]{1,0:T(8,128)(2,1)S(1)}, u32[]{:S(2)}, u32[]{:S(2)}) collective-permute-start(bf16[128,1536]{1,0:T(8,128)(2,1)S(1)} %get-tuple-element.20), channel_id=1, source_target_pairs={{0,64},{64,0},{128,192},{192,128},{256,320},{320,256},{384,448},{4... | collective-permute-start | bytes 1179656 | tf_op jit(solution)/shard_map/ppermute | solution.py:464
  86.9 2.9 %kernel_grad_other.1 = bf16[40,1536]{1,0:T(8,128)(2,1)S(1)} custom-call(s32[1]{0:T(128)} %bitcast.place_ref, s32[2]{0:T(128)S(1)} %bitcast.25, bf16[176,1536]{1,0:T(8,128)(2,1)S(1)} %collective-permute-done.message_ref.x_ref, f32[2,12,128,128]{3,2,1,0:T(8,128)S(1)} %get-tuple-element.21.dh_ref, f32[2,8,1536]{2,1,0:T(8,128)S(1)} %get-tuple-element.22.gb_ref), custom_call_target="tpu_custom_call" | custom-call | flops 12189696 | bytes 2097152 | tf_op jit(solution)/shard_map/kernel_grad_other/pallas_call | solution.py:362
  89.7 2.0 %collective-permute-start.5 = (bf16[40,1536]{1,0:T(8,128)(2,1)S(1)}, bf16[40,1536]{1,0:T(8,128)(2,1)S(1)}, u32[]{:S(2)}, u32[]{:S(2)}) collective-permute-start(bf16[40,1536]{1,0:T(8,128)(2,1)S(1)} %kernel_grad_other.1), channel_id=1, source_target_pairs={{0,64},{64,0},{128,192},{192,128},{256,320},{320,256},{384,448},{4... | collective-permute-start | bytes 368648 | tf_op jit(solution)/shard_map/ppermute | solution.py:460
  91.7 0.0 copy-done.3
  91.7 2.8 %kernel_grad_own.1.own_ref = f32[40,1536]{1,0:T(8,128)S(1)} custom-call(s32[1]{0:T(128)} %bitcast.place_ref, s32[2]{0:T(128)S(1)} %bitcast.26, bf16[2,128,1536]{2,1,0:T(8,128)(2,1)S(1)} %bitcast.16, f32[2,12,128,128]{3,2,1,0:T(8,128)S(1)} %get-tuple-element.21.dh_ref, f32[2,8,1536]{2,1,0:T(8,128)S(1)} %get-tuple-element.22.gb_ref), custom_call_target="tpu_custom_call" | custom-call | flops 12189696 | bytes 2097152 | tf_op jit(solution)/shard_map/kernel_grad_own/pallas_call | solution.py:362
  94.5 3.1 %collective-permute-done.5.other_ref = bf16[40,1536]{1,0:T(8,128)(2,1)S(1)} collective-permute-done((bf16[40,1536]{1,0:T(8,128)(2,1)S(1)}, bf16[40,1536]{1,0:T(8,128)(2,1)S(1)}, u32[]{:S(2)}, u32[]{:S(2)}) %collective-permute-start.5) | collective-permute-done | bytes 122912 | tf_op jit(solution)/shard_map/ppermute | solution.py:460
  97.6 1.1 pack.1
  98.7 20.0 %all-to-all-start = ((bf16[64,8,128]{2,1,0:T(8,128)(2,1)}), bf16[64,8,128]{2,1,0:T(8,128)(2,1)S(1)}, u32[]{:S(2)}, u32[]{:S(2)}) async-start(bf16[64,8,128]{2,1,0:T(8,128)(2,1)} %pack.1), calls=%async_computation | async-start | bytes 262144 | tf_op jit(solution)/shard_map/all_to_all | solution.py:463
  118.7 0.0 collective-permute-done.4
  118.7 1.0 maximum_select_fusion
  119.7 16.0 %all-to-all-done.parts_ref = bf16[64,8,128]{2,1,0:T(8,128)(2,1)S(1)} async-done(((bf16[64,8,128]{2,1,0:T(8,128)(2,1)}), bf16[64,8,128]{2,1,0:T(8,128)(2,1)S(1)}, u32[]{:S(2)}, u32[]{:S(2)}) %all-to-all-start) | async-done | bytes 131104 | tf_op jit(solution)/shard_map/all_to_all | solution.py:463
  135.7 0.7 finish.1
Async XLA Ops:
  0.6 1.1 copy-start.1
  1.8 0.9 copy-start.4
  2.7 0.7 copy-start.7
  3.4 0.7 copy-start.8
  4.0 18.0 %copy-start.6 = (s32[2,1]{0,1:T(1,128)S(1)}, s32[2,1]{0,1:T(1,128)}, u32[]{:S(2)}) copy-start(s32[2,1]{0,1:T(1,128)} %param.8) | copy-start | bytes 28
  4.3 17.8 %copy-start = (bf16[2,1,128,1536]{3,2,1,0:T(8,128)(2,1)S(1)}, bf16[2,1,128,1536]{3,2,1,0:T(8,128)(2,1)}, u32[]{:S(2)}) copy-start(bf16[2,1,128,1536]{3,2,1,0:T(8,128)(2,1)} %param.7) | copy-start | bytes 2359300
  4.3 14.6 %collective-permute-start = (bf16[176,1536]{1,0:T(8,128)(2,1)S(1)}, bf16[176,1536]{1,0:T(8,128)(2,1)S(1)}, u32[]{:S(2)}, u32[]{:S(2)}) collective-permute-start(bf16[176,1536]{1,0:T(8,128)(2,1)S(1)} %get-tuple-element.16), channel_id=1, source_target_pairs={{0,64},{64,0},{128,192},{192,128},{256,320},{320,256},{384,448},{4... | collective-permute-start | bytes 1622024 | tf_op jit(solution)/shard_map/ppermute | solution.py:450
  10.1 1.1 copy-start.2
  11.2 0.7 copy-start.5
  28.8 0.7 collective-permute-start.1
  36.2 0.7 collective-permute-start.2
  43.6 31.2 %collective-permute-start.3 = (bf16[128,1536]{1,0:T(8,128)(2,1)S(1)}, bf16[128,1536]{1,0:T(8,128)(2,1)S(1)}, u32[]{:S(2)}, u32[]{:S(2)}) collective-permute-start(bf16[128,1536]{1,0:T(8,128)(2,1)S(1)} %phase.5), channel_id=1, source_target_pairs={{192,64},{128,0},{193,65},{129,1},{194,66},{130,2},{195,67},{131,3... | collective-permute-start | bytes 1179656 | tf_op jit(solution)/shard_map/ppermute | solution.py:457
  81.9 9.8 %copy-start.3 = (bf16[1,2,1,128,1536]{4,3,2,1,0:T(8,128)(2,1)S(1)}, bf16[1,2,1,128,1536]{4,3,2,1,0:T(8,128)(2,1)}, u32[]{:S(2)}) copy-start(bf16[1,2,1,128,1536]{4,3,2,1,0:T(8,128)(2,1)} %param.6) | copy-start | bytes 2359300
  81.9 36.8 %collective-permute-start.4 = (bf16[128,1536]{1,0:T(8,128)(2,1)S(1)}, bf16[128,1536]{1,0:T(8,128)(2,1)S(1)}, u32[]{:S(2)}, u32[]{:S(2)}) collective-permute-start(bf16[128,1536]{1,0:T(8,128)(2,1)S(1)} %get-tuple-element.20), channel_id=1, source_target_pairs={{0,64},{64,0},{128,192},{192,128},{256,320},{320,256},{384,448},{4... | collective-permute-start | bytes 1179656 | tf_op jit(solution)/shard_map/ppermute | solution.py:464
  89.7 7.9 %collective-permute-start.5 = (bf16[40,1536]{1,0:T(8,128)(2,1)S(1)}, bf16[40,1536]{1,0:T(8,128)(2,1)S(1)}, u32[]{:S(2)}, u32[]{:S(2)}) collective-permute-start(bf16[40,1536]{1,0:T(8,128)(2,1)S(1)} %kernel_grad_other.1), channel_id=1, source_target_pairs={{0,64},{64,0},{128,192},{192,128},{256,320},{320,256},{384,448},{4... | collective-permute-start | bytes 368648 | tf_op jit(solution)/shard_map/ppermute | solution.py:460
  98.7 37.1 %all-to-all-start = ((bf16[64,8,128]{2,1,0:T(8,128)(2,1)}), bf16[64,8,128]{2,1,0:T(8,128)(2,1)S(1)}, u32[]{:S(2)}, u32[]{:S(2)}) async-start(bf16[64,8,128]{2,1,0:T(8,128)(2,1)} %pack.1), calls=%async_computation | async-start | bytes 262144 | tf_op jit(solution)/shard_map/all_to_all | solution.py:463

commit v4 on v3

--- a/solution.py
+++ b/solution.py
@@ -14,12 +14,13 @@
 PADDED = 160
 EPS = 1e-05
 ROWS = 40
-TABLE = 48
+TABLE = 40
 F32 = jnp.float32
 BF16 = jnp.bfloat16
 VMEM = pl.BlockSpec(memory_space=pltpu.VMEM)
 SMEM = pl.BlockSpec(memory_space=pltpu.SMEM)
 ANY = pl.BlockSpec(memory_space=pl.ANY)
+HBM = pl.BlockSpec(memory_space=pltpu.HBM)
 
 
 def columns(block):
@@ -50,13 +51,24 @@
     return [high, middle, value - high - middle]
 
 
-def message_kernel(place_ref, x_ref, kernel_ref, gain_ref, bias_ref, message_ref, w_ref):
-    frames, width = x_ref.shape[1:]
+def message_kernel(place_ref, saved_hbm, kernel_hbm, gain_hbm, bias_hbm, message_ref, w_ref, x_ref, kernel_ref, gain_ref, bias_ref, sem):
+    frames, width = x_ref.shape
     filler = jnp.zeros((TABLE - KW - 6, LANES), F32)
-
-    def copy(b, carry):
-        cols = columns(b)
-        message_ref[:frames, cols] = x_ref[0, :, cols]
+    upper = upper_of(place_ref)
+    copies = [
+        pltpu.make_async_copy(kernel_hbm, kernel_ref, sem.at[0]),
+        pltpu.make_async_copy(gain_hbm, gain_ref, sem.at[1]),
+        pltpu.make_async_copy(bias_hbm, bias_ref, sem.at[2]),
+        pltpu.make_async_copy(saved_hbm.at[upper], message_ref.at[pl.ds(0, frames)], sem.at[3]),
+        pltpu.make_async_copy(saved_hbm.at[1 - upper], x_ref, sem.at[4]),
+    ]
+    for copy in copies:
+        copy.start()
+    for copy in copies[:3]:
+        copy.wait()
+
+    def tabulate(b, carry):
+        cols = columns(b)
         kernel = kernel_ref[:, cols].astype(F32)
         gain, bias = gain_ref[:, cols], bias_ref[:, cols]
         table = jnp.concatenate([kernel] + thirds(gain) + thirds(bias) + [filler], 0)
@@ -64,7 +76,9 @@
         w_ref[:, cols] = jnp.concatenate([kernel, gain, bias], 0)
         return carry
 
-    lax.fori_loop(0, width // LANES, copy, 0)
+    lax.fori_loop(0, width // LANES, tabulate, 0)
+    for copy in copies[3:]:
+        copy.wait()
 
 
 def whole(*shape):
@@ -75,20 +89,18 @@
     frames, width = saved.shape[1:]
     return pl.pallas_call(
         message_kernel,
-        grid_spec=pltpu.PrefetchScalarGridSpec(
-            num_scalar_prefetch=1,
-            grid=(1,),
-            in_specs=[
-                pl.BlockSpec((1, frames, width), lambda i, p: (lax.rem(p[0], 2), 0, 0)),
-                whole(KW, width),
-                whole(1, width),
-                whole(1, width),
-            ],
-            out_specs=[whole(frames + TABLE, width), whole(KW + 2, width)],
-        ),
+        in_specs=[SMEM, HBM, HBM, HBM, HBM],
+        out_specs=[VMEM, VMEM, VMEM],
         out_shape=[
             jax.ShapeDtypeStruct((frames + TABLE, width), BF16),
             jax.ShapeDtypeStruct((KW + 2, width), F32),
+            jax.ShapeDtypeStruct((frames, width), BF16),
+        ],
+        scratch_shapes=[
+            pltpu.VMEM((KW, width), BF16),
+            pltpu.VMEM((1, width), F32),
+            pltpu.VMEM((1, width), F32),
+            pltpu.SemaphoreType.DMA((5,)),
         ],
         compiler_params=pltpu.CompilerParams(vmem_limit_bytes=limit),
         cost_estimate=pl.CostEstimate(flops=width * 400, bytes_accessed=1 << 20, transcendentals=0),
@@ -111,7 +123,7 @@
 
 
 def forward_local_kernel(place_ref, lens_ref, x_ref, w_ref, s_ref, pad_ref):
-    forward_body(lens_ref[1 - upper_of(place_ref)], x_ref.at[0], w_ref, s_ref, pad_ref)
+    forward_body(lens_ref[1 - upper_of(place_ref)], x_ref, w_ref, s_ref, pad_ref)
 
 
 def forward_other_kernel(place_ref, lens_ref, message_ref, s_ref, w_ref, pad_ref):
@@ -158,7 +170,7 @@
 
 
 def forward(place, lens, x, w, limit=16 << 20):
-    frames, width = (x.shape[0] - TABLE, x.shape[1]) if w is None else x.shape[1:]
+    frames, width = (x.shape[0] - TABLE, x.shape[1]) if w is None else x.shape
     blocks = width // LANES
     stats = (2 * blocks + 1, frames, LANES)
     if w is None:
@@ -168,10 +180,7 @@
         out_shape = [jax.ShapeDtypeStruct(stats, F32), jax.ShapeDtypeStruct((KW + 2, width), F32)]
     else:
         body, operands = forward_local_kernel, (x, w)
-        in_specs = [
-            pl.BlockSpec((1, frames, width), lambda i, p, n: (1 - lax.rem(p[0], 2), 0, 0)),
-            whole(KW + 2, width),
-        ]
+        in_specs = [whole(frames, width), whole(KW + 2, width)]
         out_specs = whole(*stats)
         out_shape = jax.ShapeDtypeStruct(stats, F32)
     return pl.pallas_call(
@@ -335,8 +344,7 @@
 
     def correlate(b, carry):
         cols = columns(b)
-        x = x_ref[:frames, cols] if len(x_ref.shape) == 2 else x_ref[0, :, cols]
-        pad_ref[b, LEAD : LEAD + frames, :] = jnp.where(mask, x.astype(F32), 0.0)
+        pad_ref[b, LEAD : LEAD + frames, :] = jnp.where(mask, x_ref[:frames, cols].astype(F32), 0.0)
         dh = dh_ref[0, b]
         sums = []
         for j in range(KW):
@@ -354,10 +362,8 @@
     blocks, frames = dh.shape[1:3]
     width = blocks * LANES
     if own:
-        x_spec = pl.BlockSpec((1, frames, width), lambda i, p, n: (1 - lax.rem(p[0], 2), 0, 0))
         which = lambda p: 1 - lax.rem(p[0], 2)
     else:
-        x_spec = whole(*x.shape)
         which = lambda p: lax.rem(p[0], 2)
     return pl.pallas_call(
         kernel_grad_kernel,
@@ -365,7 +371,7 @@
             num_scalar_prefetch=2,
             grid=(1,),
             in_specs=[
-                x_spec,
+                whole(*x.shape),
                 pl.BlockSpec((1, blocks, frames, LANES), lambda i, p, n: (which(p), 0, 0, 0)),
                 pl.BlockSpec((1, 8, width), lambda i, p, n: (which(p), 0, 0)),
             ],
@@ -445,11 +451,10 @@
     lens = lengths[:, 0]
     stages = sections // 2
     swap = [(p, p ^ 1) for p in range(sections)]
-    saved = saved[0, :, 0]
-    sent, w_local = message(place, saved, kernel[0], gain, bias)
+    sent, w_local, x_local = message(place, saved[0, :, 0], kernel[0], gain, bias)
     came = lax.ppermute(sent, "pipe", swap)
     dys = [out_grad[:, 0]]
-    s_local = forward(place, lens, saved, w_local)
+    s_local = forward(place, lens, x_local, w_local)
     s_other, w_other = forward(place, lens, came, None)
     for k in range(stages - 1):
         (dx,) = phase(place, lens, stages, dys, s_local, s_other, w_local, w_other, False)
@@ -458,7 +463,7 @@
     own, give, gb, dh = phase(place, lens, stages, dys, s_local, s_other, w_local, w_other, True)
     kg_give = kernel_grad(place, lens, came, dh, gb, False)
     kg_other = lax.ppermute(kg_give, "pipe", swap)
-    kg_own = kernel_grad(place, lens, saved, dh, gb, True)
+    kg_own = kernel_grad(place, lens, x_local, dh, gb, True)
     packed = pack(kg_own, kg_other, members)
     parts = lax.all_to_all(packed, "dp", 0, 0, tiled=True)
     dx_other = lax.ppermute(give, "pipe", swap)

time: 137 us -> 137 us (level)
    unnamed x18 -> x14, local copies, waits for them, and re-layouts: 5.2 us -> 4.06 us
where the time goes in v4:
time: 137 us; the launch traced here: 136 us
  waiting for transfers between devices  53.5 us (39%)
  Pallas kernels  41.6 us (30%)
  starting transfers between devices  35.1 us (26%)
  local copies, waits for them, and re-layouts  4.06 us (3%)
    ppermute x3, waiting for transfers between devices, local(): dys.append(lax.ppermute(dx, 'pipe', [(top, top - 2), (top - 1, top - 3)]))  29.9 us
    pallas_call x4, Pallas kernels, phase(): pl.pallas_call(functools.partial(phase_kernel, len(dys), last, stages), o...  27.2 us
    all_to_all x1, starting transfers between devices, local(): parts = lax.all_to_all(packed, 'dp', 0, 0, tiled=True)  20 us
    all_to_all x1, waiting for transfers between devices, local(): parts = lax.all_to_all(packed, 'dp', 0, 0, tiled=True)  16 us
    pallas_call x2, Pallas kernels, forward(): pl.pallas_call(body, grid_spec=pltpu.PrefetchScalarGridSpec(num_scalar_pr...  6.23 us
    pallas_call x2, Pallas kernels, kernel_grad(): pl.pallas_call(kernel_grad_kernel, grid_spec=pltpu.PrefetchScalarGridSpec...  5.68 us
    ppermute x1, starting transfers between devices, local(): came = lax.ppermute(sent, 'pipe', swap)  5.64 us
    ppermute x1, starting transfers between devices, local(): dx_other = lax.ppermute(give, 'pipe', swap)  4.82 us
  transfers between devices with their start and end apart: 7, of which 4 were waited for; matrix products, arithmetic and copies ran while one was open for 1% of the time, Pallas kernels for 7%

profile of v4, /device:TPU:1, one launch (start us, length us, event | category | flops | bytes accessed | tf_op | source)
XLA Modules:
  0.0 136.1 jit_solution(18379014596489207035)
XLA Ops:
  0.6 0.0 copy-start.1
  0.6 1.1 copy-done.1
  1.8 0.0 copy-start.2
  1.8 0.9 copy-done.2
  2.7 0.0 copy-start.5
  2.7 0.7 copy-done.5
  3.4 0.0 copy-start.6
  3.4 0.7 copy-done.6
  4.0 0.0 copy-start
  4.1 0.7 message.1
  4.8 5.6 %collective-permute-start = (bf16[168,1536]{1,0:T(8,128)(2,1)S(1)}, bf16[168,1536]{1,0:T(8,128)(2,1)S(1)}, u32[]{:S(2)}, u32[]{:S(2)}) collective-permute-start(bf16[168,1536]{1,0:T(8,128)(2,1)S(1)} %get-tuple-element.18), channel_id=1, source_target_pairs={{0,64},{64,0},{128,192},{192,128},{256,320},{320,256},{384,448},{4... | collective-permute-start | bytes 1548296 | tf_op jit(solution)/shard_map/ppermute | solution.py:455
  10.4 0.0 copy-start.3
  10.4 0.6 copy-done.3
  11.1 3.1 %forward_local.1.refs_1_.refs_2_.refs_3_.refs_4_ = f32[25,128,128]{2,1,0:T(8,128)S(1)} custom-call(s32[1]{0:T(128)} %bitcast.place_ref, s32[2]{0:T(128)S(1)} %bitcast.17, bf16[128,1536]{1,0:T(8,128)(2,1)S(1)} %get-tuple-element.16.x_ref, f32[33,1536]{1,0:T(8,128)S(1)} %get-tuple-element.17.w_ref.refs_3_.refs_4_.refs_5_.refs_6_), custom_call_target="tpu_custom_call" | custom-call | flops 19660800 | bytes 3145728 | tf_op jit(solution)/shard_map/forward_local/pallas_call | solution.py:186
  14.1 4.5 %collective-permute-done.message_ref.x_ref = bf16[168,1536]{1,0:T(8,128)(2,1)S(1)} collective-permute-done((bf16[168,1536]{1,0:T(8,128)(2,1)S(1)}, bf16[168,1536]{1,0:T(8,128)(2,1)S(1)}, u32[]{:S(2)}, u32[]{:S(2)}) %collective-permute-start) | collective-permute-done | bytes 516128 | tf_op jit(solution)/shard_map/ppermute | solution.py:455
  18.7 3.2 %forward_other.1 = (f32[25,128,128]{2,1,0:T(8,128)S(1)}, f32[33,1536]{1,0:T(8,128)S(1)}) custom-call(s32[1]{0:T(128)} %bitcast.place_ref, s32[2]{0:T(128)S(1)} %bitcast.18, bf16[168,1536]{1,0:T(8,128)(2,1)S(1)} %collective-permute-done.message_ref.x_ref), custom_call_target="tpu_custom_call" | custom-call | flops 19660800 | bytes 3145728 | tf_op jit(solution)/shard_map/forward_other/pallas_call | solution.py:186
  21.8 0.0 copy-done
  21.8 6.7 %phase.3 = bf16[128,1536]{1,0:T(8,128)(2,1)S(1)} custom-call(s32[1]{0:T(128)} %bitcast.place_ref, s32[2]{0:T(128)S(1)} %bitcast.19, bf16[2,128,1536]{2,1,0:T(8,128)(2,1)S(1)} %bitcast.10, f32[25,128,128]{2,1,0:T(8,128)S(1)} %forward_local.1.refs_1_.refs_2_.refs_3_.refs_4_, f32[25,128,128]{2,1,0:T(8,128)S(1)} %get-tuple-element.19.refs_2_.refs_3_.refs_4_.refs_5_, ...), custom_call_target="tpu_custom_call" | custom-call | flops 31457280 | bytes 5242880 | tf_op jit(solution)/shard_map/phase/pallas_call | solution.py:326
  28.5 0.7 collective-permute-start.1
  29.2 0.0 collective-permute-done.1.refs_1_
  29.3 6.7 %phase.4 = bf16[128,1536]{1,0:T(8,128)(2,1)S(1)} custom-call(s32[1]{0:T(128)} %bitcast.place_ref, s32[2]{0:T(128)S(1)} %bitcast.20, bf16[2,128,1536]{2,1,0:T(8,128)(2,1)S(1)} %bitcast.11, bf16[128,1536]{1,0:T(8,128)(2,1)S(1)} %collective-permute-done.1.refs_1_, f32[25,128,128]{2,1,0:T(8,128)S(1)} %forward_local.1.refs_1_.refs_2_.refs_3_.refs_4_, ...), custom_call_target="tpu_custom_call" | custom-call | flops 31457280 | bytes 5242880 | tf_op jit(solution)/shard_map/phase/pallas_call | solution.py:326
  36.0 0.7 collective-permute-start.2
  36.7 0.0 collective-permute-done.2.refs_2_
  36.7 6.7 %phase.5 = bf16[128,1536]{1,0:T(8,128)(2,1)S(1)} custom-call(s32[1]{0:T(128)} %bitcast.place_ref, s32[2]{0:T(128)S(1)} %bitcast.21, bf16[2,128,1536]{2,1,0:T(8,128)(2,1)S(1)} %bitcast.12, bf16[128,1536]{1,0:T(8,128)(2,1)S(1)} %collective-permute-done.1.refs_1_, bf16[128,1536]{1,0:T(8,128)(2,1)S(1)} %collective-permute-done.2.refs_2_, ...), custom_call_target="tpu_custom_call" | custom-call | flops 31457280 | bytes 5242880 | tf_op jit(solution)/shard_map/phase/pallas_call | solution.py:326
  43.4 1.3 collective-permute-start.3
  44.7 29.9 %collective-permute-done.3.refs_3_ = bf16[128,1536]{1,0:T(8,128)(2,1)S(1)} collective-permute-done((bf16[128,1536]{1,0:T(8,128)(2,1)S(1)}, bf16[128,1536]{1,0:T(8,128)(2,1)S(1)}, u32[]{:S(2)}, u32[]{:S(2)}) %collective-permute-start.3) | collective-permute-done | bytes 393248 | tf_op jit(solution)/shard_map/ppermute | solution.py:462
  74.6 7.1 %phase_last.1 = (bf16[128,1536]{1,0:T(8,128)(2,1)S(1)}, bf16[128,1536]{1,0:T(8,128)(2,1)S(1)}, f32[2,8,1536]{2,1,0:T(8,128)S(1)}, f32[2,12,128,128]{3,2,1,0:T(8,128)S(1)}) custom-call(s32[1]{0:T(128)} %bitcast.place_ref, s32[2]{0:T(128)S(1)} %bitcast.22, bf16[2,128,1536]{2,1,0:T(8,128)(2,1)S(1)} %bitcast.13, ...), custom_call_target="tpu_custom_call" | custom-call | flops 31457280 | bytes 5242880 | tf_op jit(solution)/shard_map/phase_last/pallas_call | solution.py:326
  81.7 0.0 copy-start.4
  81.7 4.8 %collective-permute-start.4 = (bf16[128,1536]{1,0:T(8,128)(2,1)S(1)}, bf16[128,1536]{1,0:T(8,128)(2,1)S(1)}, u32[]{:S(2)}, u32[]{:S(2)}) collective-permute-start(bf16[128,1536]{1,0:T(8,128)(2,1)S(1)} %get-tuple-element.22), channel_id=1, source_target_pairs={{0,64},{64,0},{128,192},{192,128},{256,320},{320,256},{384,448},{4... | collective-permute-start | bytes 1179656 | tf_op jit(solution)/shard_map/ppermute | solution.py:469
  86.5 2.9 %kernel_grad_other.1 = bf16[40,1536]{1,0:T(8,128)(2,1)S(1)} custom-call(s32[1]{0:T(128)} %bitcast.place_ref, s32[2]{0:T(128)S(1)} %bitcast.23, bf16[168,1536]{1,0:T(8,128)(2,1)S(1)} %collective-permute-done.message_ref.x_ref, f32[2,12,128,128]{3,2,1,0:T(8,128)S(1)} %get-tuple-element.23.dh_ref, f32[2,8,1536]{2,1,0:T(8,128)S(1)} %get-tuple-element.24.gb_ref), custom_call_target="tpu_custom_call" | custom-call | flops 12189696 | bytes 2097152 | tf_op jit(solution)/shard_map/kernel_grad_other/pallas_call | solution.py:368
  89.4 2.0 %collective-permute-start.5 = (bf16[40,1536]{1,0:T(8,128)(2,1)S(1)}, bf16[40,1536]{1,0:T(8,128)(2,1)S(1)}, u32[]{:S(2)}, u32[]{:S(2)}) collective-permute-start(bf16[40,1536]{1,0:T(8,128)(2,1)S(1)} %kernel_grad_other.1), channel_id=1, source_target_pairs={{0,64},{64,0},{128,192},{192,128},{256,320},{320,256},{384,448},{4... | collective-permute-start | bytes 368648 | tf_op jit(solution)/shard_map/ppermute | solution.py:465
  91.3 0.0 copy-done.4
  91.4 2.8 %kernel_grad_own.1.own_ref = f32[40,1536]{1,0:T(8,128)S(1)} custom-call(s32[1]{0:T(128)} %bitcast.place_ref, s32[2]{0:T(128)S(1)} %bitcast.24, bf16[128,1536]{1,0:T(8,128)(2,1)S(1)} %get-tuple-element.16.x_ref, f32[2,12,128,128]{3,2,1,0:T(8,128)S(1)} %get-tuple-element.23.dh_ref, f32[2,8,1536]{2,1,0:T(8,128)S(1)} %get-tuple-element.24.gb_ref), custom_call_target="tpu_custom_call" | custom-call | flops 12189696 | bytes 2097152 | tf_op jit(solution)/shard_map/kernel_grad_own/pallas_call | solution.py:368
  94.2 3.1 %collective-permute-done.5.other_ref = bf16[40,1536]{1,0:T(8,128)(2,1)S(1)} collective-permute-done((bf16[40,1536]{1,0:T(8,128)(2,1)S(1)}, bf16[40,1536]{1,0:T(8,128)(2,1)S(1)}, u32[]{:S(2)}, u32[]{:S(2)}) %collective-permute-start.5) | collective-permute-done | bytes 122912 | tf_op jit(solution)/shard_map/ppermute | solution.py:465
  97.2 1.1 pack.1
  98.3 20.0 %all-to-all-start = ((bf16[64,8,128]{2,1,0:T(8,128)(2,1)}), bf16[64,8,128]{2,1,0:T(8,128)(2,1)S(1)}, u32[]{:S(2)}, u32[]{:S(2)}) async-start(bf16[64,8,128]{2,1,0:T(8,128)(2,1)} %pack.1), calls=%async_computation | async-start | bytes 262144 | tf_op jit(solution)/shard_map/all_to_all | solution.py:468
  118.3 0.0 collective-permute-done.4
  118.4 1.0 maximum_select_fusion
  119.4 16.0 %all-to-all-done.parts_ref = bf16[64,8,128]{2,1,0:T(8,128)(2,1)S(1)} async-done(((bf16[64,8,128]{2,1,0:T(8,128)(2,1)}), bf16[64,8,128]{2,1,0:T(8,128)(2,1)S(1)}, u32[]{:S(2)}, u32[]{:S(2)}) %all-to-all-start) | async-done | bytes 131104 | tf_op jit(solution)/shard_map/all_to_all | solution.py:468
  135.4 0.7 finish.1
Async XLA Ops:
  0.6 1.1 copy-start.1
  1.8 0.9 copy-start.2
  2.7 0.7 copy-start.5
  3.4 0.7 copy-start.6
  4.0 17.8 %copy-start = (bf16[2,1,128,1536]{3,2,1,0:T(8,128)(2,1)S(1)}, bf16[2,1,128,1536]{3,2,1,0:T(8,128)(2,1)}, u32[]{:S(2)}) copy-start(bf16[2,1,128,1536]{3,2,1,0:T(8,128)(2,1)} %param.7) | copy-start | bytes 2359300
  4.8 13.9 %collective-permute-start = (bf16[168,1536]{1,0:T(8,128)(2,1)S(1)}, bf16[168,1536]{1,0:T(8,128)(2,1)S(1)}, u32[]{:S(2)}, u32[]{:S(2)}) collective-permute-start(bf16[168,1536]{1,0:T(8,128)(2,1)S(1)} %get-tuple-element.18), channel_id=1, source_target_pairs={{0,64},{64,0},{128,192},{192,128},{256,320},{320,256},{384,448},{4... | collective-permute-start | bytes 1548296 | tf_op jit(solution)/shard_map/ppermute | solution.py:455
  10.4 0.7 copy-start.3
  28.5 0.7 collective-permute-start.1
  36.0 0.7 collective-permute-start.2
  43.4 31.2 %collective-permute-start.3 = (bf16[128,1536]{1,0:T(8,128)(2,1)S(1)}, bf16[128,1536]{1,0:T(8,128)(2,1)S(1)}, u32[]{:S(2)}, u32[]{:S(2)}) collective-permute-start(bf16[128,1536]{1,0:T(8,128)(2,1)S(1)} %phase.5), channel_id=1, source_target_pairs={{192,64},{128,0},{193,65},{129,1},{194,66},{130,2},{195,67},{131,3... | collective-permute-start | bytes 1179656 | tf_op jit(solution)/shard_map/ppermute | solution.py:462
  81.7 9.7 %copy-start.4 = (s32[2,1]{0,1:T(1,128)S(1)}, s32[2,1]{0,1:T(1,128)}, u32[]{:S(2)}) copy-start(s32[2,1]{0,1:T(1,128)} %param.8) | copy-start | bytes 28
  81.7 36.7 %collective-permute-start.4 = (bf16[128,1536]{1,0:T(8,128)(2,1)S(1)}, bf16[128,1536]{1,0:T(8,128)(2,1)S(1)}, u32[]{:S(2)}, u32[]{:S(2)}) collective-permute-start(bf16[128,1536]{1,0:T(8,128)(2,1)S(1)} %get-tuple-element.22), channel_id=1, source_target_pairs={{0,64},{64,0},{128,192},{192,128},{256,320},{320,256},{384,448},{4... | collective-permute-start | bytes 1179656 | tf_op jit(solution)/shard_map/ppermute | solution.py:469
  89.4 7.9 %collective-permute-start.5 = (bf16[40,1536]{1,0:T(8,128)(2,1)S(1)}, bf16[40,1536]{1,0:T(8,128)(2,1)S(1)}, u32[]{:S(2)}, u32[]{:S(2)}) collective-permute-start(bf16[40,1536]{1,0:T(8,128)(2,1)S(1)} %kernel_grad_other.1), channel_id=1, source_target_pairs={{0,64},{64,0},{128,192},{192,128},{256,320},{320,256},{384,448},{4... | collective-permute-start | bytes 368648 | tf_op jit(solution)/shard_map/ppermute | solution.py:465
  98.3 37.1 %all-to-all-start = ((bf16[64,8,128]{2,1,0:T(8,128)(2,1)}), bf16[64,8,128]{2,1,0:T(8,128)(2,1)S(1)}, u32[]{:S(2)}, u32[]{:S(2)}) async-start(bf16[64,8,128]{2,1,0:T(8,128)(2,1)} %pack.1), calls=%async_computation | async-start | bytes 262144 | tf_op jit(solution)/shard_map/all_to_all | solution.py:468
